TPU v7x, 512 devices: a whole 4x8x8 slice. The times are simulated.
512 devices in a mesh: gz: 32 (over x_hi, z, core), gy: 16 (over x_lo, y).
Axes of the slice: x: 4 (x_hi: 2, x_lo: 2; x = x_hi * 2 + x_lo), y: 8, z: 8, core: 2. Of those that a mesh axis runs over, the one named last changes fastest.
Arguments:
- tokens: bfloat16 [1, 64, 32, 64, 512], P(None, 'gz', 'gy'), may hold values from -75 to 75
- w_qkv: bfloat16 [512, 1536], replicated, may hold values from -0.25 to 0.25
- w_out: bfloat16 [512, 512], replicated, may hold values from -0.25 to 0.25
- rel_bias: float32 [16, 5, 5, 5], replicated, may hold values from -4 to 4
- gain: float32 [512], replicated, may hold values from 0.5 to 1.5
Outputs:
- update: bfloat16 [1, 64, 32, 64, 512], P(None, 'gz', 'gy')
All inputs are finite; a program needn't handle non-finite values.
Results may differ from a plain program's by a relative error of at most 0.0079.
Values may be sent and summed in bfloat16 or wider, within the bound.
No kernel may reach another device: no remote copies, remote signals or barrier semaphores. Data moves between devices by JAX's collectives and lax.ppermute only.
A program may use at most 128 MiB of HBM per device.

v0:
```python
import jax
import jax.numpy as jnp
from jax import lax
from jax.sharding import PartitionSpec as P

DILATION_DEPTH = 8


def shifted(block, axis, distance):
    devices = range(lax.axis_size(axis))
    route = [((i - distance) % len(devices), i) for i in devices]
    return lax.ppermute(block, axis, route)


def pick_rows(y_rows, per_row):
    chosen = 1
    for candidate in range(1, y_rows + 1):
        if y_rows % candidate == 0 and candidate * per_row <= 1024:
            chosen = candidate
    return chosen


def collect_planes(key_value, depth_stride, kernel_radius):
    axis_count = lax.axis_size("gz")
    received = {0: key_value}
    for offset in range(-kernel_radius, kernel_radius + 1):
        if offset != 0:
            distance = -offset * depth_stride % axis_count
            received[offset] = shifted(key_value, "gz", distance)
    return jnp.stack([received[offset] for offset in range(-kernel_radius, kernel_radius + 1)], 0)


def neighbourhood(queries, padded, bias_part):
    boxes, depth_planes, y_rows, x_cells, local_heads, head_dim = queries.shape
    kernel = padded.shape[0]
    kernel_radius = kernel // 2
    score_scale = float(head_dim) ** (-0.5)
    block_rows = pick_rows(y_rows, local_heads * x_cells)
    row_blocks = y_rows // block_rows
    block_count = boxes * depth_planes * row_blocks

    def tap_window(wide, tap_y):
        rows_part = wide[:, tap_y : tap_y + block_rows]
        return jnp.stack([rows_part[:, :, tap_x : tap_x + x_cells] for tap_x in range(kernel)], 1)

    def one_block(block_index):
        slab_index = block_index // row_blocks
        row_start = block_index % row_blocks * block_rows
        box_index = slab_index // depth_planes
        depth_plane_index = slab_index % depth_planes
        query_block = lax.dynamic_slice(
            queries,
            (box_index, depth_plane_index, row_start, 0, 0, 0),
            (1, 1, block_rows, x_cells, local_heads, head_dim),
        )[0, 0]
        pair_block = lax.dynamic_slice(
            padded,
            (0, box_index, depth_plane_index, row_start, 0, 0, 0, 0),
            (kernel, 1, 1, block_rows + 2 * kernel_radius, x_cells, local_heads, 2, head_dim),
        )[:, 0, 0]
        wide = jnp.concatenate(
            [
                pair_block[:, :, x_cells - kernel_radius :],
                pair_block,
                pair_block[:, :, :kernel_radius],
            ],
            axis=2,
        )
        score_parts = []
        for tap_y in range(kernel):
            window = tap_window(wide, tap_y)
            score_parts.append(
                jnp.einsum(
                    "yxhd,abyxhd->yhxab",
                    query_block,
                    window[..., 0, :],
                    preferred_element_type=jnp.float32,
                )
            )
        scores = jnp.stack(score_parts, 4) * score_scale + bias_part[None, :, None]
        row_max = jnp.max(scores, axis=(3, 4, 5), keepdims=True)
        exponent = jnp.exp(scores - row_max)
        weights = (exponent / jnp.sum(exponent, axis=(3, 4, 5), keepdims=True)).astype(jnp.bfloat16)
        mixed = jnp.zeros((block_rows, x_cells, local_heads, head_dim), jnp.float32)
        for tap_y in range(kernel):
            window = tap_window(wide, tap_y)
            mixed = mixed + jnp.einsum(
                "yhxab,abyxhd->yxhd",
                weights[:, :, :, :, tap_y],
                window[..., 1, :],
                preferred_element_type=jnp.float32,
            )
        return mixed.astype(jnp.bfloat16).reshape(block_rows, x_cells, local_heads * head_dim)

    block_out = lax.map(one_block, jnp.arange(block_count, dtype=jnp.int32))
    return block_out.reshape(boxes, depth_planes, y_rows, x_cells, local_heads * head_dim)


def body(tokens, w_qkv, w_out, rel_bias, gain):
    boxes, depth_planes, y_rows, x_cells, model_width = tokens.shape
    head_count = rel_bias.shape[0]
    kernel = rel_bias.shape[1]
    kernel_radius = kernel // 2
    head_dim = model_width // head_count
    depth_stride = DILATION_DEPTH // depth_planes
    projected = jnp.dot(
        tokens.reshape(-1, model_width), w_qkv, preferred_element_type=jnp.float32
    ).astype(jnp.bfloat16)
    projected = projected.reshape(boxes, depth_planes, y_rows, x_cells, 3 * model_width)
    exchanged = lax.all_to_all(projected, "gy", split_axis=4, concat_axis=2, tiled=True)
    local_heads = exchanged.shape[-1] // (3 * head_dim)
    unpacked = exchanged.reshape(exchanged.shape[:4] + (local_heads, 3, head_dim))
    queries = unpacked[..., 0, :]
    key_value = unpacked[..., 1:, :]
    plane_taps = collect_planes(key_value, depth_stride, kernel_radius)
    padded = jnp.concatenate(
        [plane_taps[:, :, :, -kernel_radius:], plane_taps, plane_taps[:, :, :, :kernel_radius]],
        axis=3,
    )
    head_start = lax.axis_index("gy") * local_heads
    bias_part = lax.dynamic_slice_in_dim(rel_bias, head_start, local_heads, 0)
    gathered = neighbourhood(queries, padded, bias_part)
    attended = lax.all_to_all(gathered, "gy", split_axis=2, concat_axis=4, tiled=True)
    projection = jnp.dot(
        attended.reshape(-1, model_width), w_out, preferred_element_type=jnp.float32
    )
    mean_sq = jnp.mean(projection * projection, axis=-1, keepdims=True)
    update = (projection * lax.rsqrt(mean_sq + 1e-06) * gain).astype(jnp.bfloat16)
    return update.reshape(boxes, depth_planes, y_rows, x_cells, model_width)


def solution(mesh):
    in_specs = (P(None, "gz", "gy", None, None), P(), P(), P(), P())
    out_specs = P(None, "gz", "gy", None, None)
    return jax.shard_map(body, mesh=mesh, in_specs=in_specs, out_specs=out_specs, check_vma=False)
```

profile of v0, /device:TPU:6, one launch (start us, length us, event | category | flops | bytes accessed | tf_op | source)
XLA Modules:
  0.0 571.2 jit_solution(9642494151995949665)
XLA Ops:
  5.2 29.0 %all_to_all.30 = bf16[16,2,12288]{2,1,0:T(2,128)(2,1)S(1)} all-to-all(bf16[16,2,12288]{2,1,0:T(2,128)(2,1)S(1)} %reshape.447), channel_id=1, replica_groups=mesh['gz'=32,'gy'=16] {'gy'}, dimensions={0} | all-to-all | bytes 1572864 | tf_op jit(solution)/shard_map/all_to_all | solution.py:110
  35.8 10.9 %collective-permute-start = (bf16[1,2,32,64,1,2,32]{3,6,5,2,1,4,0:T(8,128)(2,1)S(1)}, bf16[1,2,32,64,1,2,32]{3,6,5,2,1,4,0:T(8,128)(2,1)}, u32[]{:S(2)}, u32[]{:S(2)}) collective-permute-start(bf16[1,2,32,64,1,2,32]{3,6,5,2,1,4,0:T(8,128)(2,1)S(1)} %slice.412), channel_id=1, source_target_pairs={{384,0},{400,16},{416,32},{432,48},{448,64},{464,80},{480,96},{496... | collective-permute-start | bytes 1572872 | tf_op jit(solution)/shard_map/ppermute | solution.py:12
  51.5 6.1 %collective-permute-start.2 = (bf16[1,2,32,64,1,2,32]{3,6,5,2,1,4,0:T(8,128)(2,1)S(1)}, bf16[1,2,32,64,1,2,32]{3,6,5,2,1,4,0:T(8,128)(2,1)S(1)}, u32[]{:S(2)}, u32[]{:S(2)}) collective-permute-start(bf16[1,2,32,64,1,2,32]{3,6,5,2,1,4,0:T(8,128)(2,1)S(1)} %slice.412), channel_id=1, source_target_pairs={{64,0},{80,16},{96,32},{112,48},{128,64},{144,80},{160,96},{176,11... | collective-permute-start | bytes 1572872 | tf_op jit(solution)/shard_map/ppermute | solution.py:12
  60.6 34.1 %collective-permute-done = bf16[1,2,32,64,1,2,32]{3,6,5,2,1,4,0:T(8,128)(2,1)} collective-permute-done((bf16[1,2,32,64,1,2,32]{3,6,5,2,1,4,0:T(8,128)(2,1)S(1)}, bf16[1,2,32,64,1,2,32]{3,6,5,2,1,4,0:T(8,128)(2,1)}, u32[]{:S(2)}, u32[]{:S(2)}) %collective-permute-start) | collective-permute-done | bytes 524320 | tf_op jit(solution)/shard_map/ppermute | solution.py:12
  95.9 26.4 %collective-permute-done.1 = bf16[1,2,32,64,1,2,32]{3,6,5,2,1,4,0:T(8,128)(2,1)S(1)} collective-permute-done((bf16[1,2,32,64,1,2,32]{3,6,5,2,1,4,0:T(8,128)(2,1)S(1)}, bf16[1,2,32,64,1,2,32]{3,6,5,2,1,4,0:T(8,128)(2,1)S(1)}, u32[]{:S(2)}, u32[]{:S(2)}) %collective-permute-start.1) | collective-permute-done | bytes 524320 | tf_op jit(solution)/shard_map/ppermute | solution.py:12
  122.7 75.1 %collective-permute-done.2 = bf16[1,2,32,64,1,2,32]{3,6,5,2,1,4,0:T(8,128)(2,1)S(1)} collective-permute-done((bf16[1,2,32,64,1,2,32]{3,6,5,2,1,4,0:T(8,128)(2,1)S(1)}, bf16[1,2,32,64,1,2,32]{3,6,5,2,1,4,0:T(8,128)(2,1)S(1)}, u32[]{:S(2)}, u32[]{:S(2)}) %collective-permute-start.2) | collective-permute-done | bytes 524320 | tf_op jit(solution)/shard_map/ppermute | solution.py:12
  202.9 345.6 %while.12 = (s32[]{:T(128)}, bf16[4,16,64,32]{3,2,1,0:T(8,128)(2,1)}, s32[4]{0:T(128)S(1)}, bf16[1,2,32,64,1,32]{3,5,4,2,1,0:T(8,128)(2,1)}, bf16[5,1,2,36,64,1,...) while((s32[]{:T(128)}, ...), condition=%wide.region_3.4_spmd, body=%wide.region_0.3_spmd.sunk | while | flops 52357156 | bytes 131976720 | solution.py:95
  215.3 5.2 fusion.63
  231.8 9.5 %slice_bitcast_fusion.24 = (bf16[16,64,5,5,32]{1,4,0,2,3:T(8,128)(2,1)}, bf16[16,64,32,5,5]{1,2,0,3,4:T(8,128)(2,1)}, bf16[16,64,32,5,5]{1,2,0,3,4:T(8,128)(2,1)}, bf16[16,64,5,5,32]{1,4,0,2,3:T(8,128)(2,1)}) fusion(bf16[5,5,16,64,1,2,32]{3,6,5,2,0,4,1:T(8,128)(2,1)} %copy-done.3, bf16[5,5,16,64,1,2,32]{3,6,5,2,0,4,1:T(8,128)(2,1)S(1)} %get-tuple-element.271), kind=kLoop, calls=%fused_computation.12.clone.1 | loop fusion | bytes 13107200 | tf_op jit(solution)/shard_map/while
  241.3 6.3 %slice_bitcast_fusion.23 = (bf16[16,64,5,5,32]{1,4,0,2,3:T(8,128)(2,1)S(1)}, bf16[16,64,32,5,5]{1,2,0,3,4:T(8,128)(2,1)}, bf16[16,64,32,5,5]{1,2,0,3,4:T(8,128)(2,1)}, bf16[16,64,5,5,32]{1,4,0,2,3:T(8,128)(2,1)}) fusion(bf16[5,5,16,64,1,2,32]{3,6,5,2,0,4,1:T(8,128)(2,1)S(1)} %get-tuple-element.265, ...), kind=kLoop, calls=%fused_computation.10.clone.1 | loop fusion | bytes 13107200 | tf_op jit(solution)/shard_map/while
  258.0 10.8 %multiply_reduce_fusion.17 = (f32[16,64,5,5]{1,0,3,2:T(8,128)S(1)}, f32[16,64,5,5]{1,0,3,2:T(8,128)S(1)}, f32[16,64,5,5]{1,0,3,2:T(8,128)S(1)}, f32[16,64,5,5]{1,0,3,2:T(8,128)S(1)}, f32[16,64,5,5]{1,0,3,2:T(8,128)S(1)}) fusion(f32[16,64,32]{1,2,0:T(8,128)S(1)} %bitcast_convert_fusion.2, bf16[16,64,32,5,5]{1,2,0,3,4:T(8,128)(2,1)} %get-tuple-element.267, ...), kind=kLoop, calls=%fused_computation.5.clone.1 | loop fusion | flops 12160000 | bytes 8835072 | tf_op jit(solution)/shard_map/while/body/eval_jaxpr/yxhd,abyxhd->yhxab/dot_general | solution.py:73
  301.7 5.2 fusion.63
  318.2 9.5 %slice_bitcast_fusion.24 = (bf16[16,64,5,5,32]{1,4,0,2,3:T(8,128)(2,1)}, bf16[16,64,32,5,5]{1,2,0,3,4:T(8,128)(2,1)}, bf16[16,64,32,5,5]{1,2,0,3,4:T(8,128)(2,1)}, bf16[16,64,5,5,32]{1,4,0,2,3:T(8,128)(2,1)}) fusion(bf16[5,5,16,64,1,2,32]{3,6,5,2,0,4,1:T(8,128)(2,1)} %copy-done.3, bf16[5,5,16,64,1,2,32]{3,6,5,2,0,4,1:T(8,128)(2,1)S(1)} %get-tuple-element.271), kind=kLoop, calls=%fused_computation.12.clone.1 | loop fusion | bytes 13107200 | tf_op jit(solution)/shard_map/while
  327.7 6.3 %slice_bitcast_fusion.23 = (bf16[16,64,5,5,32]{1,4,0,2,3:T(8,128)(2,1)S(1)}, bf16[16,64,32,5,5]{1,2,0,3,4:T(8,128)(2,1)}, bf16[16,64,32,5,5]{1,2,0,3,4:T(8,128)(2,1)}, bf16[16,64,5,5,32]{1,4,0,2,3:T(8,128)(2,1)}) fusion(bf16[5,5,16,64,1,2,32]{3,6,5,2,0,4,1:T(8,128)(2,1)S(1)} %get-tuple-element.265, ...), kind=kLoop, calls=%fused_computation.10.clone.1 | loop fusion | bytes 13107200 | tf_op jit(solution)/shard_map/while
  344.4 10.8 %multiply_reduce_fusion.17 = (f32[16,64,5,5]{1,0,3,2:T(8,128)S(1)}, f32[16,64,5,5]{1,0,3,2:T(8,128)S(1)}, f32[16,64,5,5]{1,0,3,2:T(8,128)S(1)}, f32[16,64,5,5]{1,0,3,2:T(8,128)S(1)}, f32[16,64,5,5]{1,0,3,2:T(8,128)S(1)}) fusion(f32[16,64,32]{1,2,0:T(8,128)S(1)} %bitcast_convert_fusion.2, bf16[16,64,32,5,5]{1,2,0,3,4:T(8,128)(2,1)} %get-tuple-element.267, ...), kind=kLoop, calls=%fused_computation.5.clone.1 | loop fusion | flops 12160000 | bytes 8835072 | tf_op jit(solution)/shard_map/while/body/eval_jaxpr/yxhd,abyxhd->yhxab/dot_general | solution.py:73
  388.1 5.2 fusion.63
  404.6 9.5 %slice_bitcast_fusion.24 = (bf16[16,64,5,5,32]{1,4,0,2,3:T(8,128)(2,1)}, bf16[16,64,32,5,5]{1,2,0,3,4:T(8,128)(2,1)}, bf16[16,64,32,5,5]{1,2,0,3,4:T(8,128)(2,1)}, bf16[16,64,5,5,32]{1,4,0,2,3:T(8,128)(2,1)}) fusion(bf16[5,5,16,64,1,2,32]{3,6,5,2,0,4,1:T(8,128)(2,1)} %copy-done.3, bf16[5,5,16,64,1,2,32]{3,6,5,2,0,4,1:T(8,128)(2,1)S(1)} %get-tuple-element.271), kind=kLoop, calls=%fused_computation.12.clone.1 | loop fusion | bytes 13107200 | tf_op jit(solution)/shard_map/while
  414.1 6.3 %slice_bitcast_fusion.23 = (bf16[16,64,5,5,32]{1,4,0,2,3:T(8,128)(2,1)S(1)}, bf16[16,64,32,5,5]{1,2,0,3,4:T(8,128)(2,1)}, bf16[16,64,32,5,5]{1,2,0,3,4:T(8,128)(2,1)}, bf16[16,64,5,5,32]{1,4,0,2,3:T(8,128)(2,1)}) fusion(bf16[5,5,16,64,1,2,32]{3,6,5,2,0,4,1:T(8,128)(2,1)S(1)} %get-tuple-element.265, ...), kind=kLoop, calls=%fused_computation.10.clone.1 | loop fusion | bytes 13107200 | tf_op jit(solution)/shard_map/while
  430.8 10.8 %multiply_reduce_fusion.17 = (f32[16,64,5,5]{1,0,3,2:T(8,128)S(1)}, f32[16,64,5,5]{1,0,3,2:T(8,128)S(1)}, f32[16,64,5,5]{1,0,3,2:T(8,128)S(1)}, f32[16,64,5,5]{1,0,3,2:T(8,128)S(1)}, f32[16,64,5,5]{1,0,3,2:T(8,128)S(1)}) fusion(f32[16,64,32]{1,2,0:T(8,128)S(1)} %bitcast_convert_fusion.2, bf16[16,64,32,5,5]{1,2,0,3,4:T(8,128)(2,1)} %get-tuple-element.267, ...), kind=kLoop, calls=%fused_computation.5.clone.1 | loop fusion | flops 12160000 | bytes 8835072 | tf_op jit(solution)/shard_map/while/body/eval_jaxpr/yxhd,abyxhd->yhxab/dot_general | solution.py:73
  474.5 5.2 fusion.63
  491.0 9.5 %slice_bitcast_fusion.24 = (bf16[16,64,5,5,32]{1,4,0,2,3:T(8,128)(2,1)}, bf16[16,64,32,5,5]{1,2,0,3,4:T(8,128)(2,1)}, bf16[16,64,32,5,5]{1,2,0,3,4:T(8,128)(2,1)}, bf16[16,64,5,5,32]{1,4,0,2,3:T(8,128)(2,1)}) fusion(bf16[5,5,16,64,1,2,32]{3,6,5,2,0,4,1:T(8,128)(2,1)} %copy-done.3, bf16[5,5,16,64,1,2,32]{3,6,5,2,0,4,1:T(8,128)(2,1)S(1)} %get-tuple-element.271), kind=kLoop, calls=%fused_computation.12.clone.1 | loop fusion | bytes 13107200 | tf_op jit(solution)/shard_map/while
  500.5 6.3 %slice_bitcast_fusion.23 = (bf16[16,64,5,5,32]{1,4,0,2,3:T(8,128)(2,1)S(1)}, bf16[16,64,32,5,5]{1,2,0,3,4:T(8,128)(2,1)}, bf16[16,64,32,5,5]{1,2,0,3,4:T(8,128)(2,1)}, bf16[16,64,5,5,32]{1,4,0,2,3:T(8,128)(2,1)}) fusion(bf16[5,5,16,64,1,2,32]{3,6,5,2,0,4,1:T(8,128)(2,1)S(1)} %get-tuple-element.265, ...), kind=kLoop, calls=%fused_computation.10.clone.1 | loop fusion | bytes 13107200 | tf_op jit(solution)/shard_map/while
  517.2 10.8 %multiply_reduce_fusion.17 = (f32[16,64,5,5]{1,0,3,2:T(8,128)S(1)}, f32[16,64,5,5]{1,0,3,2:T(8,128)S(1)}, f32[16,64,5,5]{1,0,3,2:T(8,128)S(1)}, f32[16,64,5,5]{1,0,3,2:T(8,128)S(1)}, f32[16,64,5,5]{1,0,3,2:T(8,128)S(1)}) fusion(f32[16,64,32]{1,2,0:T(8,128)S(1)} %bitcast_convert_fusion.2, bf16[16,64,32,5,5]{1,2,0,3,4:T(8,128)(2,1)} %get-tuple-element.267, ...), kind=kLoop, calls=%fused_computation.5.clone.1 | loop fusion | flops 12160000 | bytes 8835072 | tf_op jit(solution)/shard_map/while/body/eval_jaxpr/yxhd,abyxhd->yhxab/dot_general | solution.py:73
  550.5 18.1 %all_to_all.31 = bf16[16,2,4096]{2,1,0:T(2,128)(2,1)S(1)} all-to-all(bf16[16,2,4096]{2,1,0:T(2,128)(2,1)S(1)} %reshape.449), channel_id=1, replica_groups=mesh['gz'=32,'gy'=16] {'gy'}, dimensions={0} | all-to-all | bytes 524288 | tf_op jit(solution)/shard_map/all_to_all | solution.py:123
  (212 shorter events, 232.5 us)
Async XLA Ops:
  35.2 11.5 %copy-start.7 = (f32[16,5,5,5]{0,3,2,1:T(8,128)S(1)}, f32[16,5,5,5]{0,3,2,1:T(8,128)}, u32[]{:S(2)}) copy-start(f32[16,5,5,5]{0,3,2,1:T(8,128)} %param.10) | copy-start | bytes 24004
  35.8 58.8 %collective-permute-start = (bf16[1,2,32,64,1,2,32]{3,6,5,2,1,4,0:T(8,128)(2,1)S(1)}, bf16[1,2,32,64,1,2,32]{3,6,5,2,1,4,0:T(8,128)(2,1)}, u32[]{:S(2)}, u32[]{:S(2)}) collective-permute-start(bf16[1,2,32,64,1,2,32]{3,6,5,2,1,4,0:T(8,128)(2,1)S(1)} %slice.412), channel_id=1, source_target_pairs={{384,0},{400,16},{416,32},{432,48},{448,64},{464,80},{480,96},{496... | collective-permute-start | bytes 1572872 | tf_op jit(solution)/shard_map/ppermute | solution.py:12
  47.2 75.2 %collective-permute-start.1 = (bf16[1,2,32,64,1,2,32]{3,6,5,2,1,4,0:T(8,128)(2,1)S(1)}, bf16[1,2,32,64,1,2,32]{3,6,5,2,1,4,0:T(8,128)(2,1)S(1)}, u32[]{:S(2)}, u32[]{:S(2)}) collective-permute-start(bf16[1,2,32,64,1,2,32]{3,6,5,2,1,4,0:T(8,128)(2,1)S(1)} %slice.412), channel_id=1, source_target_pairs={{448,0},{464,16},{480,32},{496,48},{0,64},{16,80},{32,96},{48,112}... | collective-permute-start | bytes 1572872 | tf_op jit(solution)/shard_map/ppermute | solution.py:12
  51.5 146.4 %collective-permute-start.2 = (bf16[1,2,32,64,1,2,32]{3,6,5,2,1,4,0:T(8,128)(2,1)S(1)}, bf16[1,2,32,64,1,2,32]{3,6,5,2,1,4,0:T(8,128)(2,1)S(1)}, u32[]{:S(2)}, u32[]{:S(2)}) collective-permute-start(bf16[1,2,32,64,1,2,32]{3,6,5,2,1,4,0:T(8,128)(2,1)S(1)} %slice.412), channel_id=1, source_target_pairs={{64,0},{80,16},{96,32},{112,48},{128,64},{144,80},{160,96},{176,11... | collective-permute-start | bytes 1572872 | tf_op jit(solution)/shard_map/ppermute | solution.py:12
  57.5 140.4 %collective-permute-start.3 = (bf16[1,2,32,64,1,2,32]{3,6,5,2,1,4,0:T(8,128)(2,1)S(1)}, bf16[1,2,32,64,1,2,32]{3,6,5,2,1,4,0:T(8,128)(2,1)S(1)}, u32[]{:S(2)}, u32[]{:S(2)}) collective-permute-start(bf16[1,2,32,64,1,2,32]{3,6,5,2,1,4,0:T(8,128)(2,1)S(1)} %slice.412), channel_id=1, source_target_pairs={{128,0},{144,16},{160,32},{176,48},{192,64},{208,80},{224,96},{240... | collective-permute-start | bytes 1572872 | tf_op jit(solution)/shard_map/ppermute | solution.py:12
  202.9 66.6 %copy-start.4 = (f32[1,5,5,5]{3,2,1,0:T(8,128)}, f32[1,5,5,5]{3,2,1,0:T(8,128)S(1)}, u32[]{:S(2)}) copy-start(f32[1,5,5,5]{3,2,1,0:T(8,128)S(1)} %get-tuple-element.320) | copy-start | bytes 1504 | tf_op jit(solution)/shard_map/while
  229.1 2.7 copy-start.3
  269.0 2.2 copy-start.2
  286.9 2.5 copy-start.5
  289.3 66.6 %copy-start.4 = (f32[1,5,5,5]{3,2,1,0:T(8,128)}, f32[1,5,5,5]{3,2,1,0:T(8,128)S(1)}, u32[]{:S(2)}) copy-start(f32[1,5,5,5]{3,2,1,0:T(8,128)S(1)} %get-tuple-element.320) | copy-start | bytes 1504 | tf_op jit(solution)/shard_map/while
  315.5 2.7 copy-start.3
  355.4 2.2 copy-start.2
  373.2 2.4 copy-start.5
  375.7 66.6 %copy-start.4 = (f32[1,5,5,5]{3,2,1,0:T(8,128)}, f32[1,5,5,5]{3,2,1,0:T(8,128)S(1)}, u32[]{:S(2)}) copy-start(f32[1,5,5,5]{3,2,1,0:T(8,128)S(1)} %get-tuple-element.320) | copy-start | bytes 1504 | tf_op jit(solution)/shard_map/while
  401.8 2.7 copy-start.3
  441.8 2.2 copy-start.2
  459.6 2.5 copy-start.5
  462.1 66.6 %copy-start.4 = (f32[1,5,5,5]{3,2,1,0:T(8,128)}, f32[1,5,5,5]{3,2,1,0:T(8,128)S(1)}, u32[]{:S(2)}) copy-start(f32[1,5,5,5]{3,2,1,0:T(8,128)S(1)} %get-tuple-element.320) | copy-start | bytes 1504 | tf_op jit(solution)/shard_map/while
  488.3 2.7 copy-start.3
  528.2 2.2 copy-start.2
  546.0 2.5 copy-start.5
  550.1 19.8 %copy-start.6 = (bf16[512,512]{1,0:T(8,128)(2,1)S(1)}, bf16[512,512]{1,0:T(8,128)(2,1)}, u32[]{:S(2)}) copy-start(bf16[512,512]{1,0:T(8,128)(2,1)} %param.9) | copy-start | bytes 1572868
  568.7 1.7 copy-start.8
  568.7 2.5 copy-start.1
  (1 other events, 1.4 us)
where the time goes:
time: 573 us; the launch traced here: 571 us
  other arithmetic  220 us (38%)
  waiting for transfers between devices  136 us (24%)
  local copies, waits for them, and re-layouts  132 us (23%)
  blocking collectives  47.2 us (8%)
  starting transfers between devices  23.4 us (4%)
  loops' own time  11.3 us (2%)
    ppermute x4, waiting for transfers between devices, shifted(): return lax.ppermute(block, axis, route)  136 us
    while x52, other arithmetic  119 us
    while x68, local copies, waits for them, and re-layouts  88.9 us
    dot_general x4, other arithmetic, one_block(): jnp.einsum('yxhd,abyxhd->yhxab', query_block, window[..., 0, :], preferre...  43.2 us
    another operation x12, other arithmetic, tap_window(): jnp.stack([rows_part[:, :, tap_x:tap_x + x_cells] for tap_x in range(kern...  38.8 us
    all_to_all x1, blocking collectives, body(): lax.all_to_all(projected, 'gy', split_axis=4, concat_axis=2, tiled=True)  29 us
    ppermute x4, starting transfers between devices, shifted(): return lax.ppermute(block, axis, route)  23.4 us
    all_to_all x1, blocking collectives, body(): lax.all_to_all(gathered, 'gy', split_axis=2, concat_axis=4, tiled=True)  18.1 us
  transfers between devices with their start and end apart: 4, of which 3 were waited for; matrix products, arithmetic and copies ran while one was open for 1% of the time, Pallas kernels for 0%

commit v1 on v0

v1 whole, which is shorter than its diff:
```python
import functools
import math

import jax
import jax.numpy as jnp
import numpy as np
from jax import lax
from jax.experimental import pallas as pl
from jax.experimental.pallas import tpu as pltpu
from jax.sharding import PartitionSpec as P


DILATION_DEPTH = 8
LOG2E = math.log2(math.e)
MASKED = -1e30
GROUP = 4
CHAINS = 64


def product_nt(a, b):
    return lax.dot_general(a, b, (((1,), (1,)), ((), ())), preferred_element_type=jnp.float32)


def shifted(block, axis, distance):
    count = lax.axis_size(axis)
    return lax.ppermute(block, axis, [((i - distance) % count, i) for i in range(count)])


def weight_kernel(head_dim, w_ref, query_ref, key_ref, value_ref):
    wide = GROUP * head_dim
    rows = lax.broadcasted_iota(jnp.int32, (wide, 3 * wide), 0)
    columns = lax.broadcasted_iota(jnp.int32, (wide, 3 * wide), 1)
    for group in range(key_ref.shape[0] // wide):
        block = w_ref[:, group * 3 * wide : (group + 1) * 3 * wide]
        for kind, ref in enumerate((query_ref, key_ref, value_ref)):
            source = (rows // head_dim) * 3 * head_dim + kind * head_dim + rows % head_dim
            pick = jnp.where(columns == source, 1.0, 0.0).astype(jnp.bfloat16)
            where = slice(group * wide, (group + 1) * wide)
            if kind == 1:
                ref[:, where] = product_nt(block, pick).astype(jnp.bfloat16)
            else:
                ref[where, :] = product_nt(pick, block).astype(jnp.bfloat16)


def split_weights(w_qkv, head_dim):
    width = w_qkv.shape[0]
    one = pltpu.VMEM((width, width), jnp.bfloat16)
    return pl.pallas_call(
        functools.partial(weight_kernel, head_dim),
        out_shape=[one] * 3,
        cost_estimate=pl.CostEstimate(
            flops=3_000_000_000, transcendentals=0, bytes_accessed=3_000_000
        ),
        name="split_weights",
    )(w_qkv)


def bias_rows(rel_bias, y_rows, cells):
    heads, taps, kernel, _ = rel_bias.shape
    radius = kernel // 2
    key_rows = y_rows + kernel - 1
    lanes = y_rows * cells
    place = np.zeros((kernel, kernel, key_rows, cells, y_rows), np.float32)
    for key_row in range(key_rows):
        for q in range(y_rows):
            if 0 <= key_row - q < kernel:
                for k in range(kernel):
                    place[key_row - q, k, key_row, (radius - k) % cells, q] = 1.0
    place = place.reshape(kernel * kernel, key_rows * lanes)
    outside = np.where(place.sum(0) > 0, 0.0, MASKED).astype(np.float32)
    rows = jnp.dot(
        rel_bias.reshape(heads * taps, kernel * kernel),
        jnp.asarray(place),
        precision=lax.Precision.HIGHEST,
    )
    return rows * LOG2E + jnp.asarray(outside)


def stage_kernel(which, kernel, cells, first, last, scale, *refs):
    refs = list(refs)
    own_ref, low_ref, high_ref, wk_ref, wv_ref, bias_ref = refs[:6]
    refs = refs[6:]
    if first:
        wq_ref = refs.pop(0)
    else:
        query_in, acc_in, max_in, sum_in = refs[:4]
        refs = refs[4:]
    if last:
        wo_ref, gain_ref, out_ref = refs[:3]
        refs = refs[3:]
    else:
        if first:
            query_out = refs.pop(0)
        acc_out, max_out, sum_out = refs[:3]
        refs = refs[3:]
    keys_ref, values_ref, score_ref, spread_ref = refs[:4]
    refs = refs[4:]
    if last:
        attended_ref = refs[0]
    query_ref = query_out if first else query_in
    taps = len(which)
    planes = own_ref.shape[0] // taps
    tokens = own_ref.shape[1]
    y_rows = tokens // cells
    head_dim = 32
    group = pl.program_id(0)

    def reorder(a, side):
        order = jnp.where(interleave, 1.0, 0.0).astype(jnp.bfloat16)
        moved = lax.dot_general(
            a, order, (((1,), (side,)), ((), ())), preferred_element_type=jnp.float32
        )
        return moved.astype(jnp.bfloat16)

    from_lane = lax.broadcasted_iota(jnp.int32, (tokens, tokens), 0)
    to_lane = lax.broadcasted_iota(jnp.int32, (tokens, tokens), 1)
    interleave = from_lane == (to_lane % y_rows) * cells + to_lane // y_rows

    @pl.when(group == 0)
    def _():
        for part, ref in enumerate((low_ref, own_ref, high_ref)):
            block = ref[...].reshape(taps * planes * tokens, ref.shape[2])
            keys = jnp.dot(block, wk_ref[...], preferred_element_type=jnp.float32)
            values = product_nt(wv_ref[...], block)
            for tap in range(taps):
                for plane in range(planes):
                    start = (tap * 3 + part) * tokens
                    at = (tap * planes + plane) * tokens
                    keys_ref[plane, start : start + tokens, :] = keys[
                        at : at + tokens
                    ].astype(jnp.bfloat16)
                    values_ref[plane, :, start : start + tokens] = values[
                        :, at : at + tokens
                    ].astype(jnp.bfloat16)
        if first:
            queries = product_nt(wq_ref[...], own_ref[...].reshape(planes * tokens, own_ref.shape[2]))
            for plane in range(planes):
                query_out[plane] = reorder(
                    queries[:, plane * tokens : (plane + 1) * tokens].astype(jnp.bfloat16), 0
                )

    wide = GROUP * head_dim
    base = pl.multiple_of(group * wide, wide)
    count = keys_ref.shape[1]
    head_of_row = lax.broadcasted_iota(jnp.int32, (wide, tokens), 0) // head_dim
    ones = jnp.ones((16, count), jnp.bfloat16)
    units = [(plane, pair) for pair in range(GROUP // 2) for plane in range(planes)]
    key_rows = count // taps // cells

    def spread(pair):
        for side in range(2):
            head = group * GROUP + 2 * pair + side
            for at, tap in enumerate(which):
                line = bias_ref[pl.ds(head * kernel + tap, 1), :]
                for key_row in range(key_rows):
                    row = line[:, key_row * tokens : (key_row + 1) * tokens]
                    start = (at * key_rows + key_row) * cells
                    spread_ref[pair % 2, side, start : start + cells, :] = pltpu.roll(
                        jnp.broadcast_to(row, (cells, tokens)),
                        0,
                        1,
                        stride=y_rows,
                        stride_axis=0,
                    )

    def score(slot, plane, pair):
        if plane == 0:
            spread(pair)
        keys = keys_ref[plane, :, pl.ds(base, wide)]
        queries = query_ref[plane, pl.ds(base, wide), :].astype(jnp.float32) * scale
        chosen = []
        for side in range(2):
            one_head = jnp.where(head_of_row == 2 * pair + side, queries, 0.0)
            coarse = one_head.astype(jnp.bfloat16)
            fine = (one_head - coarse.astype(jnp.float32)).astype(jnp.bfloat16)
            chosen.append(jnp.concatenate([coarse, fine], 0))
        dotted = jnp.dot(
            jnp.concatenate([keys, keys], 1),
            jnp.concatenate(chosen, 1),
            preferred_element_type=jnp.float32,
        )
        tops = []
        for side in range(2):
            head = 2 * pair + side
            scores = dotted[:, side * tokens : (side + 1) * tokens] + spread_ref[pair % 2, side]
            score_ref[slot, side] = scores
            top = jnp.max(scores.reshape(count // CHAINS, CHAINS, tokens), axis=0)
            top = jnp.max(top, axis=0, keepdims=True)
            if not first:
                top = jnp.maximum(top, max_in[plane, pl.ds(group * GROUP + head, 1), :])
            tops.append(top)
        return tops

    def mix(slot, plane, pair, tops):
        exponents = [
            jnp.exp2(score_ref[slot, side] - tops[side]).astype(jnp.bfloat16) for side in range(2)
        ]
        start = pl.multiple_of(base + pair * 2 * head_dim, 2 * head_dim)
        values = values_ref[plane, pl.ds(start, 2 * head_dim), :]
        mixed = jnp.dot(
            jnp.concatenate([values, ones], 0),
            jnp.concatenate(exponents, 1),
            preferred_element_type=jnp.float32,
        )
        for side in range(2):
            head = 2 * pair + side
            lanes = slice(side * tokens, (side + 1) * tokens)
            acc = mixed[side * head_dim : (side + 1) * head_dim, lanes]
            total = mixed[2 * head_dim : 2 * head_dim + 1, lanes]
            rows = pl.ds(pl.multiple_of(start + side * head_dim, head_dim), head_dim)
            one = pl.ds(group * GROUP + head, 1)
            if not first:
                shrink = jnp.exp2(max_in[plane, one, :] - tops[side])
                acc = acc + acc_in[plane, rows, :] * shrink
                total = total + sum_in[plane, one, :] * shrink
            if last:
                attended_ref[plane, rows, :] = (acc / total).astype(jnp.bfloat16)
            else:
                acc_out[plane, rows, :] = acc
                max_out[plane, one, :] = tops[side]
                sum_out[plane, one, :] = total

    waiting = score(0, *units[0])
    for index, unit in enumerate(units):
        tops = waiting
        if index + 1 < len(units):
            waiting = score((index + 1) % 2, *units[index + 1])
        mix(index % 2, *unit, tops)

    if last:

        @pl.when(group == pl.num_programs(0) - 1)
        def _():
            for plane in range(planes):
                projection = lax.dot_general(
                    reorder(attended_ref[plane], 1),
                    wo_ref[...],
                    (((0,), (0,)), ((), ())),
                    preferred_element_type=jnp.float32,
                )
                mean_sq = jnp.mean(projection * projection, axis=-1, keepdims=True)
                update = projection * lax.rsqrt(mean_sq + 1e-06) * gain_ref[...]
                out_ref[plane] = update.astype(jnp.bfloat16)


def stage(which, own, low, high, wk, wv, bias, shape, first=None, state=None, last=None):
    taps = len(which)
    tokens, width = own.shape[1:]
    planes = own.shape[0] // taps
    heads, kernel, cells = shape
    y_rows = tokens // cells
    count = (y_rows + kernel - 1) * cells * taps
    head_dim = width // heads

    def whole(a):
        rank = len(a.shape)
        return pl.BlockSpec(a.shape, lambda g: (0,) * rank)

    inputs = [own, low, high, wk, wv, bias]
    specs = [whole(a) for a in inputs]
    extra = ([first] if first is not None else list(state)) + (list(last) if last else [])
    inputs += extra
    specs += [whole(a) for a in extra]
    if last:
        outs = [jax.ShapeDtypeStruct((planes, tokens, width), jnp.bfloat16)]
    else:
        outs = [
            jax.ShapeDtypeStruct((planes, width, tokens), jnp.float32),
            jax.ShapeDtypeStruct((planes, heads, tokens), jnp.float32),
            jax.ShapeDtypeStruct((planes, heads, tokens), jnp.float32),
        ]
        if first is not None:
            outs = [jax.ShapeDtypeStruct((planes, width, tokens), jnp.bfloat16)] + outs
    scratch = [
        pltpu.VMEM((planes, count, width), jnp.bfloat16),
        pltpu.VMEM((planes, width, count), jnp.bfloat16),
        pltpu.VMEM((2, 2, count, tokens), jnp.float32),
        pltpu.VMEM((2, 2, count, tokens), jnp.float32),
    ]
    if last:
        scratch.append(pltpu.VMEM((planes, width, tokens), jnp.bfloat16))
    scale = float(head_dim) ** -0.5 * LOG2E
    return pl.pallas_call(
        functools.partial(
            stage_kernel, which, kernel, cells, first is not None, last is not None, scale
        ),
        grid=(heads // GROUP,),
        in_specs=specs,
        out_specs=[whole(a) for a in outs],
        out_shape=outs,
        scratch_shapes=scratch,
        cost_estimate=pl.CostEstimate(
            flops=taps * 1_500_000_000, transcendentals=0, bytes_accessed=taps * 4_000_000
        ),
        compiler_params=pltpu.CompilerParams(vmem_limit_bytes=24 * 1024 * 1024),
    )(*inputs)


def sublayer(tokens, w_qkv, w_out, rel_bias, gain):
    boxes, depth_planes, y_rows, cells, width = tokens.shape
    heads = rel_bias.shape[0]
    head_dim = width // heads
    stride = DILATION_DEPTH // depth_planes
    own = tokens.reshape(boxes * depth_planes, y_rows * cells, width)

    below = shifted(own, "gz", stride)
    above = shifted(own, "gz", -stride)
    low = shifted(own, "gy", 1)
    high = shifted(own, "gy", -1)
    below_two = shifted(below, "gz", stride)
    above_two = shifted(above, "gz", -stride)
    near = jnp.concatenate([below, above], 0)
    near_low = shifted(near, "gy", 1)
    near_high = shifted(near, "gy", -1)
    far = jnp.concatenate([below_two, above_two], 0)
    far_low = shifted(far, "gy", 1)
    far_high = shifted(far, "gy", -1)

    wq, wk, wv = split_weights(w_qkv, head_dim)
    bias = bias_rows(rel_bias, y_rows, cells)
    shape = (heads, rel_bias.shape[1], cells)

    query, *state = stage((2,), own, low, high, wk, wv, bias, shape, first=wq)
    state = stage((1, 3), near, near_low, near_high, wk, wv, bias, shape, state=[query] + state)
    (update,) = stage(
        (0, 4),
        far,
        far_low,
        far_high,
        wk,
        wv,
        bias,
        shape,
        state=[query] + list(state),
        last=(w_out, gain.reshape(1, width)),
    )
    return update.reshape(tokens.shape)


def solution(mesh):
    in_specs = (P(None, "gz", "gy", None, None), P(), P(), P(), P())
    out_specs = P(None, "gz", "gy", None, None)
    return jax.shard_map(sublayer, mesh=mesh, in_specs=in_specs, out_specs=out_specs, check_vma=False)
```

time: 573 us -> 82.8 us (0.14)
  the two profiles are of different devices: /device:TPU:6 before, /device:TPU:384 now
where the time goes in v1:
time: 82.8 us; the launch traced here: 82.4 us
  starting transfers between devices  39.9 us (48%)
  Pallas kernels  23.4 us (28%)
  waiting for transfers between devices  18 us (22%)
    ppermute x10, starting transfers between devices, shifted(): lax.ppermute(block, axis, [((i - distance) % count, i) for i in range(cou...  39.9 us
    pallas_call x3, Pallas kernels, stage(): pl.pallas_call(functools.partial(stage_kernel, which, kernel, cells, firs...  20.7 us
    ppermute x10, waiting for transfers between devices, shifted(): lax.ppermute(block, axis, [((i - distance) % count, i) for i in range(cou...  18 us
    pallas_call x1, Pallas kernels, split_weights(): pl.pallas_call(functools.partial(weight_kernel, head_dim), out_shape=[one...  2.69 us
  transfers between devices with their start and end apart: 10, of which 3 were waited for; matrix products, arithmetic and copies ran while one was open for 1% of the time, Pallas kernels for 17%

profile of v1, /device:TPU:384, one launch (start us, length us, event | category | flops | bytes accessed | tf_op | source)
XLA Modules:
  0.0 82.4 jit_solution(2148539261882990966)
XLA Ops:
  0.0 2.0 %collective-permute-start = (bf16[2,128,512]{2,1,0:T(8,128)(2,1)}, bf16[2,128,512]{2,1,0:T(8,128)(2,1)S(1)}, u32[]{:S(2)}, u32[]{:S(2)}) collective-permute-start(bf16[2,128,512]{2,1,0:T(8,128)(2,1)} %bitcast.11), channel_id=1, source_target_pairs={{448,0},{464,16},{480,32},{496,48},{0,64},{16,80},{32,96},{48,112}... | collective-permute-start | bytes 786440 | tf_op jit(solution)/shard_map/ppermute | solution.py:26
  2.1 3.5 %collective-permute-start.6 = (bf16[2,128,512]{2,1,0:T(8,128)(2,1)}, bf16[2,128,512]{2,1,0:T(8,128)(2,1)S(1)}, u32[]{:S(2)}, u32[]{:S(2)}) collective-permute-start(bf16[2,128,512]{2,1,0:T(8,128)(2,1)} %bitcast.12), channel_id=1, source_target_pairs={{15,0},{0,1},{1,2},{2,3},{3,4},{4,5},{5,6},{6,7},{7,8},{8,9},{9,10... | collective-permute-start | bytes 786440 | tf_op jit(solution)/shard_map/ppermute | solution.py:26
  5.5 4.7 %collective-permute-start.7 = (bf16[2,128,512]{2,1,0:T(8,128)(2,1)}, bf16[2,128,512]{2,1,0:T(8,128)(2,1)S(1)}, u32[]{:S(2)}, u32[]{:S(2)}) collective-permute-start(bf16[2,128,512]{2,1,0:T(8,128)(2,1)} %bitcast.13), channel_id=1, source_target_pairs={{1,0},{2,1},{3,2},{4,3},{5,4},{6,5},{7,6},{8,7},{9,8},{10,9},{11,1... | collective-permute-start | bytes 786440 | tf_op jit(solution)/shard_map/ppermute | solution.py:26
  10.3 4.8 %collective-permute-start.2 = (bf16[2,128,512]{2,1,0:T(8,128)(2,1)}, bf16[2,128,512]{2,1,0:T(8,128)(2,1)S(1)}, u32[]{:S(2)}, u32[]{:S(2)}) collective-permute-start(bf16[2,128,512]{2,1,0:T(8,128)(2,1)} %bitcast.14), channel_id=1, source_target_pairs={{64,0},{80,16},{96,32},{112,48},{128,64},{144,80},{160,96},{176,11... | collective-permute-start | bytes 786440 | tf_op jit(solution)/shard_map/ppermute | solution.py:26
  15.1 1.7 %collective-permute-done = bf16[2,128,512]{2,1,0:T(8,128)(2,1)S(1)} collective-permute-done((bf16[2,128,512]{2,1,0:T(8,128)(2,1)}, bf16[2,128,512]{2,1,0:T(8,128)(2,1)S(1)}, u32[]{:S(2)}, u32[]{:S(2)}) %collective-permute-start) | collective-permute-done | bytes 262176 | tf_op jit(solution)/shard_map/ppermute | solution.py:26
  16.8 7.0 %collective-permute-start.1 = (bf16[2,128,512]{2,1,0:T(8,128)(2,1)S(1)}, bf16[2,128,512]{2,1,0:T(8,128)(2,1)S(1)}, u32[]{:S(2)}, u32[]{:S(2)}) collective-permute-start(bf16[2,128,512]{2,1,0:T(8,128)(2,1)S(1)} %collective-permute-done), channel_id=1, source_target_pairs={{448,0},{464,16},{480,32},{496,48},{0,64},{16,80},{32,96},{48,112}... | collective-permute-start | bytes 786440 | tf_op jit(solution)/shard_map/ppermute | solution.py:26
  23.8 2.7 %split_weights.1 = (bf16[512,512]{1,0:T(8,128)(2,1)S(1)}, bf16[512,512]{1,0:T(8,128)(2,1)S(1)}, bf16[512,512]{1,0:T(8,128)(2,1)S(1)}) custom-call(bf16[512,1536]{1,0:T(8,128)(2,1)} %w_ref.1), custom_call_target="tpu_custom_call" | custom-call | flops 3000000000 | bytes 3000000 | tf_op jit(solution)/shard_map/split_weights/pallas_call | solution.py:48
  26.5 0.0 copy-start.5
  26.5 0.0 copy-start.1
  26.5 0.2 copy.8
  26.8 0.1 reshape.14
  26.9 3.4 %collective-permute-done.2 = bf16[2,128,512]{2,1,0:T(8,128)(2,1)S(1)} collective-permute-done((bf16[2,128,512]{2,1,0:T(8,128)(2,1)}, bf16[2,128,512]{2,1,0:T(8,128)(2,1)S(1)}, u32[]{:S(2)}, u32[]{:S(2)}) %collective-permute-start.2) | collective-permute-done | bytes 262176 | tf_op jit(solution)/shard_map/ppermute | solution.py:26
  30.3 1.9 %collective-permute-start.3 = (bf16[2,128,512]{2,1,0:T(8,128)(2,1)S(1)}, bf16[2,128,512]{2,1,0:T(8,128)(2,1)S(1)}, u32[]{:S(2)}, u32[]{:S(2)}) collective-permute-start(bf16[2,128,512]{2,1,0:T(8,128)(2,1)S(1)} %collective-permute-done.2), channel_id=1, source_target_pairs={{64,0},{80,16},{96,32},{112,48},{128,64},{144,80},{160,96},{176,11... | collective-permute-start | bytes 786440 | tf_op jit(solution)/shard_map/ppermute | solution.py:26
  32.3 1.9 %collective-permute-start.8 = (bf16[4,128,512]{2,1,0:T(8,128)(2,1)S(1)}, bf16[4,128,512]{2,1,0:T(8,128)(2,1)S(1)}, u32[]{:S(2)}, u32[]{:S(2)}) collective-permute-start(bf16[4,128,512]{2,1,0:T(8,128)(2,1)S(1)} %constant_dynamic-update-slice_fusion.2.refs_0_), channel_id=1, source_target_pairs={{15,0},{0,1},{1,2},{2,3},{3,4},{4,5},{5,6},{6,7},{7,8},{8,9},{9,10... | collective-permute-start | bytes 1572872 | tf_op jit(solution)/shard_map/ppermute | solution.py:26
  34.2 6.0 %collective-permute-start.9 = (bf16[4,128,512]{2,1,0:T(8,128)(2,1)S(1)}, bf16[4,128,512]{2,1,0:T(8,128)(2,1)S(1)}, u32[]{:S(2)}, u32[]{:S(2)}) collective-permute-start(bf16[4,128,512]{2,1,0:T(8,128)(2,1)S(1)} %constant_dynamic-update-slice_fusion.2.refs_0_), channel_id=1, source_target_pairs={{1,0},{2,1},{3,2},{4,3},{5,4},{6,5},{7,6},{8,7},{9,8},{10,9},{11,1... | collective-permute-start | bytes 1572872 | tf_op jit(solution)/shard_map/ppermute | solution.py:26
  40.3 12.9 %collective-permute-done.3 = bf16[2,128,512]{2,1,0:T(8,128)(2,1)S(1)} collective-permute-done((bf16[2,128,512]{2,1,0:T(8,128)(2,1)S(1)}, bf16[2,128,512]{2,1,0:T(8,128)(2,1)S(1)}, u32[]{:S(2)}, u32[]{:S(2)}) %collective-permute-start.3) | collective-permute-done | bytes 262176 | tf_op jit(solution)/shard_map/ppermute | solution.py:26
  53.2 1.9 %collective-permute-start.4 = (bf16[4,128,512]{2,1,0:T(8,128)(2,1)S(1)}, bf16[4,128,512]{2,1,0:T(8,128)(2,1)S(1)}, u32[]{:S(2)}, u32[]{:S(2)}) collective-permute-start(bf16[4,128,512]{2,1,0:T(8,128)(2,1)S(1)} %constant_dynamic-update-slice_fusion.refs_0_), channel_id=1, source_target_pairs={{15,0},{0,1},{1,2},{2,3},{3,4},{4,5},{5,6},{6,7},{7,8},{8,9},{9,10... | collective-permute-start | bytes 1572872 | tf_op jit(solution)/shard_map/ppermute | solution.py:26
  55.1 6.0 %collective-permute-start.5 = (bf16[4,128,512]{2,1,0:T(8,128)(2,1)S(1)}, bf16[4,128,512]{2,1,0:T(8,128)(2,1)S(1)}, u32[]{:S(2)}, u32[]{:S(2)}) collective-permute-start(bf16[4,128,512]{2,1,0:T(8,128)(2,1)S(1)} %constant_dynamic-update-slice_fusion.refs_0_), channel_id=1, source_target_pairs={{1,0},{2,1},{3,2},{4,3},{5,4},{6,5},{7,6},{8,7},{9,8},{10,9},{11,1... | collective-permute-start | bytes 1572872 | tf_op jit(solution)/shard_map/ppermute | solution.py:26
  61.2 0.4 fusion.1.refs_5_
  61.6 4.3 %shard_map.73 = (bf16[2,512,128]{2,1,0:T(8,128)(2,1)S(1)}, f32[2,512,128]{2,1,0:T(8,128)S(1)}, f32[2,16,128]{2,1,0:T(8,128)S(1)}, f32[2,16,128]{2,1,0:T(8,128)S(1)}) custom-call(bf16[2,128,512]{2,1,0:T(8,128)(2,1)S(1)} %bitcast.15, bf16[2,128,512]{2,1,0:T(8,128)(2,1)S(1)} %collective-permute-done.6.refs_1_, ...), custom_call_target="tpu_custom_call" | custom-call | flops 1500000000 | bytes 4000000 | tf_op jit(solution)/shard_map/pallas_call | solution.py:283
  66.0 0.0 copy-start
  66.0 0.0 copy-start.2
  66.0 7.4 %shard_map.74 = (f32[2,512,128]{2,1,0:T(8,128)S(1)}, f32[2,16,128]{2,1,0:T(8,128)S(1)}, f32[2,16,128]{2,1,0:T(8,128)S(1)}) custom-call(bf16[4,128,512]{2,1,0:T(8,128)(2,1)S(1)} %constant_dynamic-update-slice_fusion.2.refs_0_, bf16[4,128,512]{2,1,0:T(8,128)(2,1)S(1)} %collective-permute-done.8.refs_1_, ...), custom_call_target="tpu_custom_call" | custom-call | flops 3000000000 | bytes 8000000 | tf_op jit(solution)/shard_map/pallas_call | solution.py:283
  73.4 9.0 %shard_map.75 = bf16[2,128,512]{2,1,0:T(8,128)(2,1)} custom-call(bf16[4,128,512]{2,1,0:T(8,128)(2,1)S(1)} %constant_dynamic-update-slice_fusion.refs_0_, bf16[4,128,512]{2,1,0:T(8,128)(2,1)S(1)} %collective-permute-done.4.refs_1_, bf16[4,128,512]{2,1,0:T(8,128)(2,1)S(1)} %collective-permute-done.5.refs_2_, bf16[512,512]{1,0:T(8,128)(2,1)S(1)} %get-tuple-element.15.refs_3_, ...), custom_call_target="tpu_custom_call" | custom-call | flops 3000000000 | bytes 8000000 | tf_op jit(solution)/shard_map/pallas_call | solution.py:283
  (19 shorter events, 0.1 us)
Async XLA Ops:
  0.0 26.5 %copy-start.3 = (f32[16,5,5,5]{0,3,2,1:T(8,128)S(1)}, f32[16,5,5,5]{0,3,2,1:T(8,128)}, u32[]{:S(2)}) copy-start(f32[16,5,5,5]{0,3,2,1:T(8,128)} %param.10) | copy-start | bytes 24004
  0.0 16.8 %collective-permute-start = (bf16[2,128,512]{2,1,0:T(8,128)(2,1)}, bf16[2,128,512]{2,1,0:T(8,128)(2,1)S(1)}, u32[]{:S(2)}, u32[]{:S(2)}) collective-permute-start(bf16[2,128,512]{2,1,0:T(8,128)(2,1)} %bitcast.11), channel_id=1, source_target_pairs={{448,0},{464,16},{480,32},{496,48},{0,64},{16,80},{32,96},{48,112}... | collective-permute-start | bytes 786440 | tf_op jit(solution)/shard_map/ppermute | solution.py:26
  2.1 53.1 %collective-permute-start.6 = (bf16[2,128,512]{2,1,0:T(8,128)(2,1)}, bf16[2,128,512]{2,1,0:T(8,128)(2,1)S(1)}, u32[]{:S(2)}, u32[]{:S(2)}) collective-permute-start(bf16[2,128,512]{2,1,0:T(8,128)(2,1)} %bitcast.12), channel_id=1, source_target_pairs={{15,0},{0,1},{1,2},{2,3},{3,4},{4,5},{5,6},{6,7},{7,8},{8,9},{9,10... | collective-permute-start | bytes 786440 | tf_op jit(solution)/shard_map/ppermute | solution.py:26
  5.5 56.1 %collective-permute-start.7 = (bf16[2,128,512]{2,1,0:T(8,128)(2,1)}, bf16[2,128,512]{2,1,0:T(8,128)(2,1)S(1)}, u32[]{:S(2)}, u32[]{:S(2)}) collective-permute-start(bf16[2,128,512]{2,1,0:T(8,128)(2,1)} %bitcast.13), channel_id=1, source_target_pairs={{1,0},{2,1},{3,2},{4,3},{5,4},{6,5},{7,6},{8,7},{9,8},{10,9},{11,1... | collective-permute-start | bytes 786440 | tf_op jit(solution)/shard_map/ppermute | solution.py:26
  10.3 20.0 %collective-permute-start.2 = (bf16[2,128,512]{2,1,0:T(8,128)(2,1)}, bf16[2,128,512]{2,1,0:T(8,128)(2,1)S(1)}, u32[]{:S(2)}, u32[]{:S(2)}) collective-permute-start(bf16[2,128,512]{2,1,0:T(8,128)(2,1)} %bitcast.14), channel_id=1, source_target_pairs={{64,0},{80,16},{96,32},{112,48},{128,64},{144,80},{160,96},{176,11... | collective-permute-start | bytes 786440 | tf_op jit(solution)/shard_map/ppermute | solution.py:26
  16.8 17.4 %collective-permute-start.1 = (bf16[2,128,512]{2,1,0:T(8,128)(2,1)S(1)}, bf16[2,128,512]{2,1,0:T(8,128)(2,1)S(1)}, u32[]{:S(2)}, u32[]{:S(2)}) collective-permute-start(bf16[2,128,512]{2,1,0:T(8,128)(2,1)S(1)} %collective-permute-done), channel_id=1, source_target_pairs={{448,0},{464,16},{480,32},{496,48},{0,64},{16,80},{32,96},{48,112}... | collective-permute-start | bytes 786440 | tf_op jit(solution)/shard_map/ppermute | solution.py:26
  26.5 34.7 %copy-start.5 = (f32[768]{0:T(1024)S(1)}, f32[768]{0:T(1024)}, u32[]{:S(2)}) copy-start(f32[768]{0:T(1024)} %constant.7.clone) | copy-start | bytes 9220
  26.5 35.1 %copy-start.1 = (bf16[1,2,2,64,512]{4,3,2,1,0:T(8,128)(2,1)S(1)}, bf16[1,2,2,64,512]{4,3,2,1,0:T(8,128)(2,1)}, u32[]{:S(2)}) copy-start(bf16[1,2,2,64,512]{4,3,2,1,0:T(8,128)(2,1)} %param.7) | copy-start | bytes 786436
  26.8 34.4 %copy-start.4 = (f32[25,768]{1,0:T(8,128)S(1)}, f32[25,768]{1,0:T(8,128)}, u32[]{:S(2)}) copy-start(f32[25,768]{1,0:T(8,128)} %constant.6.clone) | copy-start | bytes 230404
  30.3 22.9 %collective-permute-start.3 = (bf16[2,128,512]{2,1,0:T(8,128)(2,1)S(1)}, bf16[2,128,512]{2,1,0:T(8,128)(2,1)S(1)}, u32[]{:S(2)}, u32[]{:S(2)}) collective-permute-start(bf16[2,128,512]{2,1,0:T(8,128)(2,1)S(1)} %collective-permute-done.2), channel_id=1, source_target_pairs={{64,0},{80,16},{96,32},{112,48},{128,64},{144,80},{160,96},{176,11... | collective-permute-start | bytes 786440 | tf_op jit(solution)/shard_map/ppermute | solution.py:26
  32.3 33.7 %collective-permute-start.8 = (bf16[4,128,512]{2,1,0:T(8,128)(2,1)S(1)}, bf16[4,128,512]{2,1,0:T(8,128)(2,1)S(1)}, u32[]{:S(2)}, u32[]{:S(2)}) collective-permute-start(bf16[4,128,512]{2,1,0:T(8,128)(2,1)S(1)} %constant_dynamic-update-slice_fusion.2.refs_0_), channel_id=1, source_target_pairs={{15,0},{0,1},{1,2},{2,3},{3,4},{4,5},{5,6},{6,7},{7,8},{8,9},{9,10... | collective-permute-start | bytes 1572872 | tf_op jit(solution)/shard_map/ppermute | solution.py:26
  34.2 31.8 %collective-permute-start.9 = (bf16[4,128,512]{2,1,0:T(8,128)(2,1)S(1)}, bf16[4,128,512]{2,1,0:T(8,128)(2,1)S(1)}, u32[]{:S(2)}, u32[]{:S(2)}) collective-permute-start(bf16[4,128,512]{2,1,0:T(8,128)(2,1)S(1)} %constant_dynamic-update-slice_fusion.2.refs_0_), channel_id=1, source_target_pairs={{1,0},{2,1},{3,2},{4,3},{5,4},{6,5},{7,6},{8,7},{9,8},{10,9},{11,1... | collective-permute-start | bytes 1572872 | tf_op jit(solution)/shard_map/ppermute | solution.py:26
  53.2 20.2 %collective-permute-start.4 = (bf16[4,128,512]{2,1,0:T(8,128)(2,1)S(1)}, bf16[4,128,512]{2,1,0:T(8,128)(2,1)S(1)}, u32[]{:S(2)}, u32[]{:S(2)}) collective-permute-start(bf16[4,128,512]{2,1,0:T(8,128)(2,1)S(1)} %constant_dynamic-update-slice_fusion.refs_0_), channel_id=1, source_target_pairs={{15,0},{0,1},{1,2},{2,3},{3,4},{4,5},{5,6},{6,7},{7,8},{8,9},{9,10... | collective-permute-start | bytes 1572872 | tf_op jit(solution)/shard_map/ppermute | solution.py:26
  55.1 18.3 %collective-permute-start.5 = (bf16[4,128,512]{2,1,0:T(8,128)(2,1)S(1)}, bf16[4,128,512]{2,1,0:T(8,128)(2,1)S(1)}, u32[]{:S(2)}, u32[]{:S(2)}) collective-permute-start(bf16[4,128,512]{2,1,0:T(8,128)(2,1)S(1)} %constant_dynamic-update-slice_fusion.refs_0_), channel_id=1, source_target_pairs={{1,0},{2,1},{3,2},{4,3},{5,4},{6,5},{7,6},{8,7},{9,8},{10,9},{11,1... | collective-permute-start | bytes 1572872 | tf_op jit(solution)/shard_map/ppermute | solution.py:26
  66.0 7.4 %copy-start = (bf16[512,512]{1,0:T(8,128)(2,1)S(1)}, bf16[512,512]{1,0:T(8,128)(2,1)}, u32[]{:S(2)}) copy-start(bf16[512,512]{1,0:T(8,128)(2,1)} %refs_10_.1) | copy-start | bytes 1572868
  66.0 7.4 %copy-start.2 = (f32[512]{0:T(512)S(1)}, f32[512]{0:T(512)}, u32[]{:S(2)}) copy-start(f32[512]{0:T(512)} %param.11) | copy-start | bytes 6148

commit v2 on v1

v2 whole, which is shorter than its diff:
```python
import functools
import math

import jax
import jax.numpy as jnp
import numpy as np
from jax import lax
from jax.experimental import pallas as pl
from jax.experimental.pallas import tpu as pltpu
from jax.sharding import PartitionSpec as P


DILATION_DEPTH = 8
LOG2E = math.log2(math.e)
MASKED = -1e30
GROUP = 4
CHUNK = 16
LIVE = 8


def product_nt(a, b):
    return lax.dot_general(a, b, (((1,), (1,)), ((), ())), preferred_element_type=jnp.float32)


def shifted(block, axis, distance):
    count = lax.axis_size(axis)
    return lax.ppermute(block, axis, [((i - distance) % count, i) for i in range(count)])


def weight_kernel(head_dim, w_ref, query_ref, key_ref, value_ref):
    wide = GROUP * head_dim
    rows = lax.broadcasted_iota(jnp.int32, (wide, 3 * wide), 0)
    columns = lax.broadcasted_iota(jnp.int32, (wide, 3 * wide), 1)
    for group in range(key_ref.shape[0] // wide):
        block = w_ref[:, group * 3 * wide : (group + 1) * 3 * wide]
        for kind, ref in enumerate((query_ref, key_ref, value_ref)):
            source = (rows // head_dim) * 3 * head_dim + kind * head_dim + rows % head_dim
            pick = jnp.where(columns == source, 1.0, 0.0).astype(jnp.bfloat16)
            where = slice(group * wide, (group + 1) * wide)
            if kind == 1:
                ref[:, where] = product_nt(block, pick).astype(jnp.bfloat16)
            else:
                ref[where, :] = product_nt(pick, block).astype(jnp.bfloat16)


def split_weights(w_qkv, head_dim):
    width = w_qkv.shape[0]
    one = pltpu.VMEM((width, width), jnp.bfloat16)
    return pl.pallas_call(
        functools.partial(weight_kernel, head_dim),
        out_shape=[one] * 3,
        cost_estimate=pl.CostEstimate(
            flops=3_000_000_000, transcendentals=0, bytes_accessed=3_000_000
        ),
        name="split_weights",
    )(w_qkv)


def bias_rows(rel_bias, y_rows):
    heads, taps, kernel, _ = rel_bias.shape
    key_rows = y_rows + kernel - 1
    lanes = GROUP * CHUNK * y_rows
    place = np.zeros((GROUP, kernel, kernel, key_rows, lanes), np.float32)
    for key_row in range(key_rows):
        for q in range(y_rows):
            if 0 <= key_row - q < kernel:
                for a in range(GROUP):
                    for k in range(kernel):
                        lane = ((a * CHUNK - k) * y_rows + q) % lanes
                        place[a, key_row - q, k, key_row, lane] = 1.0
    place = place.reshape(GROUP * kernel * kernel, key_rows * lanes)
    seen = place.sum(0).reshape(key_rows, GROUP * CHUNK, y_rows).max(1, keepdims=True)
    outside = np.broadcast_to(seen, (key_rows, GROUP * CHUNK, y_rows)).reshape(key_rows * lanes)
    outside = np.where(outside > 0, 0.0, MASKED).astype(np.float32)
    table = rel_bias.reshape(heads // GROUP, GROUP, taps, kernel * kernel).transpose(0, 2, 1, 3)
    rows = jnp.dot(
        table.reshape(heads // GROUP * taps, GROUP * kernel * kernel),
        jnp.asarray(place),
        precision=lax.Precision.HIGHEST,
    )
    return rows * LOG2E + jnp.asarray(outside)


def stage_kernel(layout, kernel, cells, first, last, scale, *refs):
    refs = list(refs)
    block_refs = refs[: len(layout)]
    wk_ref, wv_ref, bias_ref = refs[len(layout) : len(layout) + 3]
    refs = refs[len(layout) + 3 :]
    if first:
        wq_ref = refs.pop(0)
    else:
        query_in, acc_in, max_in, sum_in = refs[:4]
        refs = refs[4:]
    if last:
        wo_ref, gain_ref, out_ref = refs[:3]
        refs = refs[3:]
    else:
        if first:
            query_out = refs.pop(0)
        acc_out, max_out, sum_out = refs[:3]
        refs = refs[3:]
    token_ref, keys_ref, values_ref, score_ref, tail_ref, spread_ref = refs[:6]
    refs = refs[6:]
    if last:
        attended_ref, done_ref = refs
    query_ref = query_out if first else query_in
    planes = block_refs[0].shape[0] // len(layout[0])
    tokens = block_refs[0].shape[1]
    width = block_refs[0].shape[2]
    places = [place for group_of in layout for place in group_of]
    y_rows = tokens // cells
    chunks = cells // CHUNK
    wide = wk_ref.shape[1] // pl.num_programs(0)
    head_dim = wide // GROUP
    span = keys_ref.shape[2]
    rows = span // CHUNK
    group = pl.program_id(0)

    token = lax.broadcasted_iota(jnp.int32, (tokens, tokens), 0)
    lane = lax.broadcasted_iota(jnp.int32, (tokens, tokens), 1)
    lane_head = lane // (CHUNK * y_rows)
    lane_x = lane // y_rows % CHUNK
    same_head = token // head_dim == lane_head

    def chosen(chunk):
        x = (lane_x + chunk * CHUNK + kernel // 2) % cells
        return jnp.where(token == lane % y_rows * cells + x, 1.0, 0.0).astype(jnp.bfloat16)

    @pl.when(group == 0)
    def _():
        at = 0
        for group_of, ref in zip(layout, block_refs):
            for tap in range(len(group_of)):
                for plane in range(planes):
                    for q in range(y_rows):
                        for chunk in range(chunks):
                            start = (chunk * rows + at * y_rows + q) * CHUNK
                            source = q * cells + chunk * CHUNK
                            token_ref[plane, start : start + CHUNK, :] = ref[
                                tap * planes + plane, source : source + CHUNK, :
                            ]
                at += 1
        for plane in range(planes):
            keys = jnp.dot(token_ref[plane], wk_ref[...], preferred_element_type=jnp.float32)
            keys_ref[plane] = keys.astype(jnp.bfloat16).reshape(chunks, span, width)
            step = chunks if span % 128 == 0 else 1
            for chunk in range(0, chunks, step):
                part = token_ref[plane, chunk * span : (chunk + step) * span, :]
                values = product_nt(wv_ref[...], part).astype(jnp.bfloat16)
                for more in range(step):
                    values_ref[plane, chunk + more] = values[:, more * span : (more + 1) * span]
        if first:
            own = block_refs[0][...].reshape(planes * tokens, width)
            queries = product_nt(wq_ref[...], own).astype(jnp.bfloat16)
            for plane in range(planes):
                mine = queries[:, plane * tokens : (plane + 1) * tokens]
                for chunk in range(chunks):
                    spread = jnp.dot(mine, chosen(chunk), preferred_element_type=jnp.float32)
                    for g in range(width // wide):
                        one = jnp.where(same_head, spread[g * wide : (g + 1) * wide] * scale, 0.0)
                        coarse = one.astype(jnp.bfloat16)
                        fine = (one - coarse.astype(jnp.float32)).astype(jnp.bfloat16)
                        query_out[g, plane * chunks + chunk, :wide, :] = coarse
                        query_out[g, plane * chunks + chunk, wide:, :] = fine

    for at, (tap, part) in enumerate(places):
        line = bias_ref[pl.ds(group * kernel + tap, 1), :]
        for q in range(y_rows):
            first_lane = (part * y_rows + q) * tokens
            row = jnp.broadcast_to(line[:, first_lane : first_lane + tokens], (8, tokens))
            row = pltpu.roll(row, 0, 1, stride=y_rows, stride_axis=0)
            for up in range(0, CHUNK + LIVE, 8):
                turned = pltpu.roll(row, up * y_rows, 1) if up else row
                reach = token[:8] + up - lane_x[:8]
                inside = jnp.logical_and(reach >= 0, reach < kernel)
                spread_ref[at * y_rows + q, up : up + 8, :] = jnp.where(inside, turned, MASKED)

    base = pl.multiple_of(group * wide, wide)
    ones = jnp.ones((16, span), jnp.bfloat16)
    units = [(plane, chunk) for plane in range(planes) for chunk in range(chunks)]

    def score(slot, plane, chunk):
        unit = plane * chunks + chunk
        queries = query_ref[group, unit]
        tops = []
        keys = jnp.concatenate(
            [
                keys_ref[plane, (chunk + half) % chunks, :, pl.ds(base, wide)]
                for half in range(2)
            ],
            0,
        )
        both = jnp.dot(
            jnp.concatenate([keys, keys], 1), queries, preferred_element_type=jnp.float32
        )
        for half in range(2):
            dotted = both[half * span : (half + 1) * span].reshape(rows, CHUNK, tokens)
            if half:
                scores = dotted[:, :LIVE] + spread_ref[:, CHUNK:, :]
                tail_ref[slot] = scores
            else:
                scores = dotted + spread_ref[:, :CHUNK, :]
                score_ref[slot] = scores
            tops.append(jnp.max(scores, axis=0))
        top = jnp.maximum(jnp.maximum(tops[0][:8], tops[0][8:]), tops[1])
        top = jnp.max(top, axis=0, keepdims=True)
        if not first:
            top = jnp.maximum(top, max_in[group, unit : unit + 1, :])
        return top

    def mix(slot, plane, chunk, top):
        unit = plane * chunks + chunk
        weights, values = [], []
        for half in range(2):
            if half:
                exponents = jnp.exp2(tail_ref[slot] - top)
                exponents = jnp.concatenate([exponents, jnp.zeros_like(exponents)], 1)
            else:
                exponents = jnp.exp2(score_ref[slot] - top)
            weights.append(exponents.reshape(span, tokens).astype(jnp.bfloat16))
            part = values_ref[plane, (chunk + half) % chunks, pl.ds(base, wide), :]
            values.append(jnp.concatenate([part, ones], 0))
        if span % 128 == 0:
            weights, values = [jnp.concatenate(weights, 0)], [jnp.concatenate(values, 1)]
        mixed = sum(
            jnp.dot(v, w, preferred_element_type=jnp.float32) for v, w in zip(values, weights)
        )
        acc = mixed[:head_dim]
        for head in range(1, GROUP):
            acc = jnp.where(
                lane_head[:head_dim] == head, mixed[head * head_dim : (head + 1) * head_dim], acc
            )
        total = mixed[wide : wide + 1]
        held = slice(unit * head_dim, (unit + 1) * head_dim)
        one = slice(unit, unit + 1)
        if not first:
            shrink = jnp.exp2(max_in[group, one, :] - top)
            acc = acc + acc_in[group, held, :] * shrink
            total = total + sum_in[group, one, :] * shrink
        if last:
            done_ref[group, held, :] = acc / total
            return
        acc_out[group, held, :] = acc
        max_out[group, one, :] = top
        sum_out[group, one, :] = total

    tops = [score(slot, *unit) for slot, unit in enumerate(units)]
    for slot, unit in enumerate(units):
        mix(slot, *unit, tops[slot])

    if last:

        @pl.when(group == pl.num_programs(0) - 1)
        def _():
            order = jnp.concatenate([chosen(chunk) for chunk in range(chunks)], 1)
            for plane in range(planes):
                laid = []
                for g in range(width // wide):
                    line = []
                    for chunk in range(chunks):
                        start = (plane * chunks + chunk) * head_dim
                        mine = jnp.concatenate([done_ref[g, start : start + head_dim, :]] * GROUP, 0)
                        line.append(jnp.where(same_head, mine, 0.0).astype(jnp.bfloat16))
                    laid.append(jnp.concatenate(line, 1))
                own_rows = slice(plane * tokens, (plane + 1) * tokens)
                attended_ref[own_rows, :] = product_nt(order, jnp.concatenate(laid, 0)).astype(
                    jnp.bfloat16
                )
            projection = jnp.dot(
                attended_ref[...], wo_ref[...], preferred_element_type=jnp.float32
            )
            mean_sq = jnp.mean(projection * projection, axis=-1, keepdims=True)
            update = projection * lax.rsqrt(mean_sq + 1e-06) * gain_ref[...]
            out_ref[...] = update.astype(jnp.bfloat16).reshape(planes, tokens, width)


def stage(layout, blocks, wk, wv, bias, shape, first=None, state=None, last=None):
    tokens, width = blocks[0].shape[1:]
    planes = blocks[0].shape[0] // len(layout[0])
    heads, kernel, cells = shape
    total = sum(len(group_of) for group_of in layout)
    rows = total * (tokens // cells)
    span = rows * CHUNK
    chunks = cells // CHUNK
    groups = heads // GROUP
    head_dim = width // heads
    wide = GROUP * head_dim

    def whole(a):
        rank = len(a.shape)
        return pl.BlockSpec(a.shape, lambda g: (0,) * rank)

    inputs = list(blocks) + [wk, wv, bias]
    inputs += ([first] if first is not None else list(state)) + (list(last) if last else [])
    specs = [whole(a) for a in inputs]
    if last:
        outs = [jax.ShapeDtypeStruct((planes, tokens, width), jnp.bfloat16)]
    else:
        units = planes * chunks
        outs = [
            jax.ShapeDtypeStruct((groups, units * head_dim, tokens), jnp.float32),
            jax.ShapeDtypeStruct((groups, units, tokens), jnp.float32),
            jax.ShapeDtypeStruct((groups, units, tokens), jnp.float32),
        ]
        if first is not None:
            outs = [jax.ShapeDtypeStruct((groups, units, 2 * wide, tokens), jnp.bfloat16)] + outs
    scratch = [
        pltpu.VMEM((planes, chunks * span, width), jnp.bfloat16),
        pltpu.VMEM((planes, chunks, span, width), jnp.bfloat16),
        pltpu.VMEM((planes, chunks, width, span), jnp.bfloat16),
        pltpu.VMEM((planes * chunks, rows, CHUNK, tokens), jnp.float32),
        pltpu.VMEM((planes * chunks, rows, LIVE, tokens), jnp.float32),
        pltpu.VMEM((rows, CHUNK + LIVE, tokens), jnp.float32),
    ]
    if last:
        scratch.append(pltpu.VMEM((planes * tokens, width), jnp.bfloat16))
        scratch.append(pltpu.VMEM((groups, planes * chunks * head_dim, tokens), jnp.float32))
    scale = float(head_dim) ** -0.5 * LOG2E
    return pl.pallas_call(
        functools.partial(
            stage_kernel, layout, kernel, cells, first is not None, last is not None, scale
        ),
        grid=(groups,),
        in_specs=specs,
        out_specs=[whole(a) for a in outs],
        out_shape=outs,
        scratch_shapes=scratch,
        cost_estimate=pl.CostEstimate(
            flops=total * 500_000_000, transcendentals=0, bytes_accessed=total * 1_300_000
        ),
        compiler_params=pltpu.CompilerParams(vmem_limit_bytes=28 * 1024 * 1024),
    )(*inputs)


def sublayer(tokens, w_qkv, w_out, rel_bias, gain):
    boxes, depth_planes, y_rows, cells, width = tokens.shape
    heads = rel_bias.shape[0]
    head_dim = width // heads
    stride = DILATION_DEPTH // depth_planes
    own = tokens.reshape(boxes * depth_planes, y_rows * cells, width)

    below = shifted(own, "gz", stride)
    above = shifted(own, "gz", -stride)
    low = shifted(own, "gy", 1)
    high = shifted(own, "gy", -1)
    below_two = shifted(below, "gz", stride)
    above_two = shifted(above, "gz", -stride)
    near = jnp.concatenate([below, above], 0)
    near_low = shifted(near, "gy", 1)
    near_high = shifted(near, "gy", -1)
    far = jnp.concatenate([below_two, above_two], 0)
    far_low = shifted(far, "gy", 1)
    far_high = shifted(far, "gy", -1)

    wq, wk, wv = split_weights(w_qkv, head_dim)
    bias = bias_rows(rel_bias, y_rows)
    shape = (heads, rel_bias.shape[1], cells)

    given = (wk, wv, bias, shape)
    query, *state = stage(
        (((2, 1),), ((2, 0),), ((2, 2),), ((1, 1), (3, 1))),
        (own, low, high, near),
        *given,
        first=wq,
    )
    state = stage(
        (((1, 0), (3, 0)), ((1, 2), (3, 2)), ((0, 1), (4, 1))),
        (near_low, near_high, far),
        *given,
        state=[query] + state,
    )
    (update,) = stage(
        (((0, 0), (4, 0)), ((0, 2), (4, 2))),
        (far_low, far_high),
        *given,
        state=[query] + list(state),
        last=(w_out, gain.reshape(1, width)),
    )
    return update.reshape(tokens.shape)


def solution(mesh):
    in_specs = (P(None, "gz", "gy", None, None), P(), P(), P(), P())
    out_specs = P(None, "gz", "gy", None, None)
    return jax.shard_map(sublayer, mesh=mesh, in_specs=in_specs, out_specs=out_specs, check_vma=False)
```

time: 82.8 us -> 78.2 us (0.944)
  the two profiles are of different devices: /device:TPU:384 before, /device:TPU:120 now
where the time goes in v2:
time: 78.2 us; the launch traced here: 77.8 us
  starting transfers between devices  44.1 us (56%)
  Pallas kernels  19.9 us (25%)
  waiting for transfers between devices  10.7 us (14%)
  local copies, waits for them, and re-layouts  2.48 us (3%)
    ppermute x10, starting transfers between devices, shifted(): lax.ppermute(block, axis, [((i - distance) % count, i) for i in range(cou...  44.1 us
    pallas_call x3, Pallas kernels, stage(): pl.pallas_call(functools.partial(stage_kernel, layout, kernel, cells, fir...  17.2 us
    ppermute x10, waiting for transfers between devices, shifted(): lax.ppermute(block, axis, [((i - distance) % count, i) for i in range(cou...  10.7 us
    pallas_call x1, Pallas kernels, split_weights(): pl.pallas_call(functools.partial(weight_kernel, head_dim), out_shape=[one...  2.69 us
  transfers between devices with their start and end apart: 10, of which 4 were waited for; matrix products, arithmetic and copies ran while one was open for 4% of the time, Pallas kernels for 19%

profile of v2, /device:TPU:120, one launch (start us, length us, event | category | flops | bytes accessed | tf_op | source)
XLA Modules:
  0.0 77.8 jit_solution(11460365709452072619)
XLA Ops:
  0.0 6.1 %collective-permute-start = (bf16[2,128,512]{2,1,0:T(8,128)(2,1)}, bf16[2,128,512]{2,1,0:T(8,128)(2,1)S(1)}, u32[]{:S(2)}, u32[]{:S(2)}) collective-permute-start(bf16[2,128,512]{2,1,0:T(8,128)(2,1)} %bitcast.11), channel_id=1, source_target_pairs={{448,0},{464,16},{480,32},{496,48},{0,64},{16,80},{32,96},{48,112}... | collective-permute-start | bytes 786440 | tf_op jit(solution)/shard_map/ppermute | solution.py:27
  6.1 8.3 %collective-permute-start.2 = (bf16[2,128,512]{2,1,0:T(8,128)(2,1)}, bf16[2,128,512]{2,1,0:T(8,128)(2,1)S(1)}, u32[]{:S(2)}, u32[]{:S(2)}) collective-permute-start(bf16[2,128,512]{2,1,0:T(8,128)(2,1)} %bitcast.12), channel_id=1, source_target_pairs={{64,0},{80,16},{96,32},{112,48},{128,64},{144,80},{160,96},{176,11... | collective-permute-start | bytes 786440 | tf_op jit(solution)/shard_map/ppermute | solution.py:27
  14.4 1.9 %collective-permute-start.6 = (bf16[2,128,512]{2,1,0:T(8,128)(2,1)}, bf16[2,128,512]{2,1,0:T(8,128)(2,1)S(1)}, u32[]{:S(2)}, u32[]{:S(2)}) collective-permute-start(bf16[2,128,512]{2,1,0:T(8,128)(2,1)} %bitcast.13), channel_id=1, source_target_pairs={{15,0},{0,1},{1,2},{2,3},{3,4},{4,5},{5,6},{6,7},{7,8},{8,9},{9,10... | collective-permute-start | bytes 786440 | tf_op jit(solution)/shard_map/ppermute | solution.py:27
  16.4 3.9 %collective-permute-start.7 = (bf16[2,128,512]{2,1,0:T(8,128)(2,1)}, bf16[2,128,512]{2,1,0:T(8,128)(2,1)S(1)}, u32[]{:S(2)}, u32[]{:S(2)}) collective-permute-start(bf16[2,128,512]{2,1,0:T(8,128)(2,1)} %bitcast.14), channel_id=1, source_target_pairs={{1,0},{2,1},{3,2},{4,3},{5,4},{6,5},{7,6},{8,7},{9,8},{10,9},{11,1... | collective-permute-start | bytes 786440 | tf_op jit(solution)/shard_map/ppermute | solution.py:27
  20.3 5.8 %collective-permute-done = bf16[2,128,512]{2,1,0:T(8,128)(2,1)S(1)} collective-permute-done((bf16[2,128,512]{2,1,0:T(8,128)(2,1)}, bf16[2,128,512]{2,1,0:T(8,128)(2,1)S(1)}, u32[]{:S(2)}, u32[]{:S(2)}) %collective-permute-start) | collective-permute-done | bytes 262176 | tf_op jit(solution)/shard_map/ppermute | solution.py:27
  26.1 1.9 %collective-permute-start.1 = (bf16[2,128,512]{2,1,0:T(8,128)(2,1)S(1)}, bf16[2,128,512]{2,1,0:T(8,128)(2,1)}, u32[]{:S(2)}, u32[]{:S(2)}) collective-permute-start(bf16[2,128,512]{2,1,0:T(8,128)(2,1)S(1)} %collective-permute-done), channel_id=1, source_target_pairs={{448,0},{464,16},{480,32},{496,48},{0,64},{16,80},{32,96},{48,112}... | collective-permute-start | bytes 786440 | tf_op jit(solution)/shard_map/ppermute | solution.py:27
  28.0 2.7 %split_weights.1 = (bf16[512,512]{1,0:T(8,128)(2,1)S(1)}, bf16[512,512]{1,0:T(8,128)(2,1)S(1)}, bf16[512,512]{1,0:T(8,128)(2,1)S(1)}) custom-call(bf16[512,1536]{1,0:T(8,128)(2,1)} %w_ref.1), custom_call_target="tpu_custom_call" | custom-call | flops 3000000000 | bytes 3000000 | tf_op jit(solution)/shard_map/split_weights/pallas_call | solution.py:49
  30.7 0.0 copy-start.3
  30.7 1.1 %reshape.21 = f32[4,4,5,25]{1,0,3,2:T(4,128)S(1)} reshape(f32[16,5,5,5]{0,3,2,1:T(8,128)} %param.10) | data formatting | bytes 16000 | tf_op jit(solution)/shard_map/reshape | solution.py:75
  31.8 0.2 copy.9
  32.1 0.1 reshape.18
  32.2 8.5 %collective-permute-start.3 = (bf16[2,128,512]{2,1,0:T(8,128)(2,1)S(1)}, bf16[2,128,512]{2,1,0:T(8,128)(2,1)S(1)}, u32[]{:S(2)}, u32[]{:S(2)}) collective-permute-start(bf16[2,128,512]{2,1,0:T(8,128)(2,1)S(1)} %collective-permute-done.2), channel_id=1, source_target_pairs={{64,0},{80,16},{96,32},{112,48},{128,64},{144,80},{160,96},{176,11... | collective-permute-start | bytes 786440 | tf_op jit(solution)/shard_map/ppermute | solution.py:27
  40.7 3.8 %collective-permute-start.8 = (bf16[4,128,512]{2,1,0:T(8,128)(2,1)S(1)}, bf16[4,128,512]{2,1,0:T(8,128)(2,1)S(1)}, u32[]{:S(2)}, u32[]{:S(2)}) collective-permute-start(bf16[4,128,512]{2,1,0:T(8,128)(2,1)S(1)} %constant_dynamic-update-slice_fusion.2.refs_3_), channel_id=1, source_target_pairs={{15,0},{0,1},{1,2},{2,3},{3,4},{4,5},{5,6},{6,7},{7,8},{8,9},{9,10... | collective-permute-start | bytes 1572872 | tf_op jit(solution)/shard_map/ppermute | solution.py:27
  44.5 2.1 %collective-permute-start.9 = (bf16[4,128,512]{2,1,0:T(8,128)(2,1)S(1)}, bf16[4,128,512]{2,1,0:T(8,128)(2,1)S(1)}, u32[]{:S(2)}, u32[]{:S(2)}) collective-permute-start(bf16[4,128,512]{2,1,0:T(8,128)(2,1)S(1)} %constant_dynamic-update-slice_fusion.2.refs_3_), channel_id=1, source_target_pairs={{1,0},{2,1},{3,2},{4,3},{5,4},{6,5},{7,6},{8,7},{9,8},{10,9},{11,1... | collective-permute-start | bytes 1572872 | tf_op jit(solution)/shard_map/ppermute | solution.py:27
  46.5 1.0 %constant_dynamic-update-slice_fusion.1 = bf16[4,128,512]{2,1,0:T(8,128)(2,1)S(1)} fusion(bf16[2,128,512]{2,1,0:T(8,128)(2,1)} %collective-permute-done.1), kind=kLoop, calls=%fused_computation.4 | loop fusion | bytes 524288
  47.5 0.2 collective-permute-done.3
  47.7 5.7 %collective-permute-start.4 = (bf16[4,128,512]{2,1,0:T(8,128)(2,1)S(1)}, bf16[4,128,512]{2,1,0:T(8,128)(2,1)S(1)}, u32[]{:S(2)}, u32[]{:S(2)}) collective-permute-start(bf16[4,128,512]{2,1,0:T(8,128)(2,1)S(1)} %constant_dynamic-update-slice_fusion.refs_2_), channel_id=1, source_target_pairs={{15,0},{0,1},{1,2},{2,3},{3,4},{4,5},{5,6},{6,7},{7,8},{8,9},{9,10... | collective-permute-start | bytes 1572872 | tf_op jit(solution)/shard_map/ppermute | solution.py:27
  53.4 1.9 %collective-permute-start.5 = (bf16[4,128,512]{2,1,0:T(8,128)(2,1)S(1)}, bf16[4,128,512]{2,1,0:T(8,128)(2,1)S(1)}, u32[]{:S(2)}, u32[]{:S(2)}) collective-permute-start(bf16[4,128,512]{2,1,0:T(8,128)(2,1)S(1)} %constant_dynamic-update-slice_fusion.refs_2_), channel_id=1, source_target_pairs={{1,0},{2,1},{3,2},{4,3},{5,4},{6,5},{7,6},{8,7},{9,8},{10,9},{11,1... | collective-permute-start | bytes 1572872 | tf_op jit(solution)/shard_map/ppermute | solution.py:27
  55.4 0.3 fusion.1.refs_6_.refs_5_.refs_4_
  55.7 6.1 %shard_map.73 = (bf16[4,8,256,128]{3,2,1,0:T(8,128)(2,1)S(1)}, f32[4,256,128]{2,1,0:T(8,128)S(1)}, f32[4,8,128]{2,1,0:T(8,128)S(1)}, f32[4,8,128]{2,1,0:T(8,128)S(1)}) custom-call(bf16[2,128,512]{2,1,0:T(8,128)(2,1)S(1)} %bitcast.15, bf16[2,128,512]{2,1,0:T(8,128)(2,1)S(1)} %collective-permute-done.6.refs_1_, ...), custom_call_target="tpu_custom_call" | custom-call | flops 2500000000 | bytes 6500000 | tf_op jit(solution)/shard_map/pallas_call | solution.py:319
  61.8 1.4 %collective-permute-done.9.refs_1_ = bf16[4,128,512]{2,1,0:T(8,128)(2,1)S(1)} collective-permute-done((bf16[4,128,512]{2,1,0:T(8,128)(2,1)S(1)}, bf16[4,128,512]{2,1,0:T(8,128)(2,1)S(1)}, u32[]{:S(2)}, u32[]{:S(2)}) %collective-permute-start.9) | collective-permute-done | bytes 524320 | tf_op jit(solution)/shard_map/ppermute | solution.py:27
  63.3 5.7 %shard_map.74 = (f32[4,256,128]{2,1,0:T(8,128)S(1)}, f32[4,8,128]{2,1,0:T(8,128)S(1)}, f32[4,8,128]{2,1,0:T(8,128)S(1)}) custom-call(bf16[4,128,512]{2,1,0:T(8,128)(2,1)S(1)} %collective-permute-done.8.refs_0_, bf16[4,128,512]{2,1,0:T(8,128)(2,1)S(1)} %collective-permute-done.9.refs_1_, bf16[4,128,512]{2,1,0:T(8,128)(2,1)S(1)} %constant_dynamic-update-slice_fusion.refs_2_, ...), custom_call_target="tpu_custom_call" | custom-call | flops 3000000000 | bytes 7800000 | tf_op jit(solution)/shard_map/pallas_call | solution.py:319
  69.0 3.3 %collective-permute-done.5.refs_1_ = bf16[4,128,512]{2,1,0:T(8,128)(2,1)S(1)} collective-permute-done((bf16[4,128,512]{2,1,0:T(8,128)(2,1)S(1)}, bf16[4,128,512]{2,1,0:T(8,128)(2,1)S(1)}, u32[]{:S(2)}, u32[]{:S(2)}) %collective-permute-start.5) | collective-permute-done | bytes 524320 | tf_op jit(solution)/shard_map/ppermute | solution.py:27
  72.3 5.4 %shard_map.75 = bf16[2,128,512]{2,1,0:T(8,128)(2,1)} custom-call(bf16[4,128,512]{2,1,0:T(8,128)(2,1)S(1)} %collective-permute-done.4.refs_0_, bf16[4,128,512]{2,1,0:T(8,128)(2,1)S(1)} %collective-permute-done.5.refs_1_, bf16[512,512]{1,0:T(8,128)(2,1)S(1)} %get-tuple-element.15.refs_4_.refs_3_.refs_2_, ...), custom_call_target="tpu_custom_call" | custom-call | flops 2000000000 | bytes 5200000 | tf_op jit(solution)/shard_map/pallas_call | solution.py:319
  (18 shorter events, 0.1 us)
Async XLA Ops:
  0.0 26.1 %collective-permute-start = (bf16[2,128,512]{2,1,0:T(8,128)(2,1)}, bf16[2,128,512]{2,1,0:T(8,128)(2,1)S(1)}, u32[]{:S(2)}, u32[]{:S(2)}) collective-permute-start(bf16[2,128,512]{2,1,0:T(8,128)(2,1)} %bitcast.11), channel_id=1, source_target_pairs={{448,0},{464,16},{480,32},{496,48},{0,64},{16,80},{32,96},{48,112}... | collective-permute-start | bytes 786440 | tf_op jit(solution)/shard_map/ppermute | solution.py:27
  6.1 26.1 %collective-permute-start.2 = (bf16[2,128,512]{2,1,0:T(8,128)(2,1)}, bf16[2,128,512]{2,1,0:T(8,128)(2,1)S(1)}, u32[]{:S(2)}, u32[]{:S(2)}) collective-permute-start(bf16[2,128,512]{2,1,0:T(8,128)(2,1)} %bitcast.12), channel_id=1, source_target_pairs={{64,0},{80,16},{96,32},{112,48},{128,64},{144,80},{160,96},{176,11... | collective-permute-start | bytes 786440 | tf_op jit(solution)/shard_map/ppermute | solution.py:27
  14.4 39.0 %collective-permute-start.6 = (bf16[2,128,512]{2,1,0:T(8,128)(2,1)}, bf16[2,128,512]{2,1,0:T(8,128)(2,1)S(1)}, u32[]{:S(2)}, u32[]{:S(2)}) collective-permute-start(bf16[2,128,512]{2,1,0:T(8,128)(2,1)} %bitcast.13), channel_id=1, source_target_pairs={{15,0},{0,1},{1,2},{2,3},{3,4},{4,5},{5,6},{6,7},{7,8},{8,9},{9,10... | collective-permute-start | bytes 786440 | tf_op jit(solution)/shard_map/ppermute | solution.py:27
  16.4 39.3 %collective-permute-start.7 = (bf16[2,128,512]{2,1,0:T(8,128)(2,1)}, bf16[2,128,512]{2,1,0:T(8,128)(2,1)S(1)}, u32[]{:S(2)}, u32[]{:S(2)}) collective-permute-start(bf16[2,128,512]{2,1,0:T(8,128)(2,1)} %bitcast.14), channel_id=1, source_target_pairs={{1,0},{2,1},{3,2},{4,3},{5,4},{6,5},{7,6},{8,7},{9,8},{10,9},{11,1... | collective-permute-start | bytes 786440 | tf_op jit(solution)/shard_map/ppermute | solution.py:27
  26.1 18.4 %collective-permute-start.1 = (bf16[2,128,512]{2,1,0:T(8,128)(2,1)S(1)}, bf16[2,128,512]{2,1,0:T(8,128)(2,1)}, u32[]{:S(2)}, u32[]{:S(2)}) collective-permute-start(bf16[2,128,512]{2,1,0:T(8,128)(2,1)S(1)} %collective-permute-done), channel_id=1, source_target_pairs={{448,0},{464,16},{480,32},{496,48},{0,64},{16,80},{32,96},{48,112}... | collective-permute-start | bytes 786440 | tf_op jit(solution)/shard_map/ppermute | solution.py:27
  30.7 24.7 %copy-start.3 = (f32[100,768]{1,0:T(8,128)S(1)}, f32[100,768]{1,0:T(8,128)}, u32[]{:S(2)}) copy-start(f32[100,768]{1,0:T(8,128)} %constant.6.clone) | copy-start | bytes 921604
  30.7 24.7 %copy-start.4 = (f32[768]{0:T(1024)S(1)}, f32[768]{0:T(1024)}, u32[]{:S(2)}) copy-start(f32[768]{0:T(1024)} %constant.7.clone) | copy-start | bytes 9220
  30.7 25.0 %copy-start.1 = (bf16[1,2,2,64,512]{4,3,2,1,0:T(8,128)(2,1)S(1)}, bf16[1,2,2,64,512]{4,3,2,1,0:T(8,128)(2,1)}, u32[]{:S(2)}) copy-start(bf16[1,2,2,64,512]{4,3,2,1,0:T(8,128)(2,1)} %param.7) | copy-start | bytes 786436
  32.2 15.5 %collective-permute-start.3 = (bf16[2,128,512]{2,1,0:T(8,128)(2,1)S(1)}, bf16[2,128,512]{2,1,0:T(8,128)(2,1)S(1)}, u32[]{:S(2)}, u32[]{:S(2)}) collective-permute-start(bf16[2,128,512]{2,1,0:T(8,128)(2,1)S(1)} %collective-permute-done.2), channel_id=1, source_target_pairs={{64,0},{80,16},{96,32},{112,48},{128,64},{144,80},{160,96},{176,11... | collective-permute-start | bytes 786440 | tf_op jit(solution)/shard_map/ppermute | solution.py:27
  40.7 21.1 %collective-permute-start.8 = (bf16[4,128,512]{2,1,0:T(8,128)(2,1)S(1)}, bf16[4,128,512]{2,1,0:T(8,128)(2,1)S(1)}, u32[]{:S(2)}, u32[]{:S(2)}) collective-permute-start(bf16[4,128,512]{2,1,0:T(8,128)(2,1)S(1)} %constant_dynamic-update-slice_fusion.2.refs_3_), channel_id=1, source_target_pairs={{15,0},{0,1},{1,2},{2,3},{3,4},{4,5},{5,6},{6,7},{7,8},{8,9},{9,10... | collective-permute-start | bytes 1572872 | tf_op jit(solution)/shard_map/ppermute | solution.py:27
  44.5 18.8 %collective-permute-start.9 = (bf16[4,128,512]{2,1,0:T(8,128)(2,1)S(1)}, bf16[4,128,512]{2,1,0:T(8,128)(2,1)S(1)}, u32[]{:S(2)}, u32[]{:S(2)}) collective-permute-start(bf16[4,128,512]{2,1,0:T(8,128)(2,1)S(1)} %constant_dynamic-update-slice_fusion.2.refs_3_), channel_id=1, source_target_pairs={{1,0},{2,1},{3,2},{4,3},{5,4},{6,5},{7,6},{8,7},{9,8},{10,9},{11,1... | collective-permute-start | bytes 1572872 | tf_op jit(solution)/shard_map/ppermute | solution.py:27
  47.7 21.3 %collective-permute-start.4 = (bf16[4,128,512]{2,1,0:T(8,128)(2,1)S(1)}, bf16[4,128,512]{2,1,0:T(8,128)(2,1)S(1)}, u32[]{:S(2)}, u32[]{:S(2)}) collective-permute-start(bf16[4,128,512]{2,1,0:T(8,128)(2,1)S(1)} %constant_dynamic-update-slice_fusion.refs_2_), channel_id=1, source_target_pairs={{15,0},{0,1},{1,2},{2,3},{3,4},{4,5},{5,6},{6,7},{7,8},{8,9},{9,10... | collective-permute-start | bytes 1572872 | tf_op jit(solution)/shard_map/ppermute | solution.py:27
  53.4 18.9 %collective-permute-start.5 = (bf16[4,128,512]{2,1,0:T(8,128)(2,1)S(1)}, bf16[4,128,512]{2,1,0:T(8,128)(2,1)S(1)}, u32[]{:S(2)}, u32[]{:S(2)}) collective-permute-start(bf16[4,128,512]{2,1,0:T(8,128)(2,1)S(1)} %constant_dynamic-update-slice_fusion.refs_2_), channel_id=1, source_target_pairs={{1,0},{2,1},{3,2},{4,3},{5,4},{6,5},{7,6},{8,7},{9,8},{10,9},{11,1... | collective-permute-start | bytes 1572872 | tf_op jit(solution)/shard_map/ppermute | solution.py:27
  63.3 9.1 %copy-start = (bf16[512,512]{1,0:T(8,128)(2,1)S(1)}, bf16[512,512]{1,0:T(8,128)(2,1)}, u32[]{:S(2)}) copy-start(bf16[512,512]{1,0:T(8,128)(2,1)} %refs_9_.1) | copy-start | bytes 1572868
  63.3 9.1 %copy-start.2 = (f32[512]{0:T(512)S(1)}, f32[512]{0:T(512)}, u32[]{:S(2)}) copy-start(f32[512]{0:T(512)} %param.11) | copy-start | bytes 6148

commit v3 on v2

--- a/solution.py
+++ b/solution.py
@@ -358,14 +358,14 @@
 
     given = (wk, wv, bias, shape)
     query, *state = stage(
-        (((2, 1),), ((2, 0),), ((2, 2),), ((1, 1), (3, 1))),
-        (own, low, high, near),
+        (((2, 1),), ((2, 0),), ((2, 2),)),
+        (own, low, high),
         *given,
         first=wq,
     )
     state = stage(
-        (((1, 0), (3, 0)), ((1, 2), (3, 2)), ((0, 1), (4, 1))),
-        (near_low, near_high, far),
+        (((1, 0), (3, 0)), ((1, 2), (3, 2)), ((0, 1), (4, 1)), ((1, 1), (3, 1))),
+        (near_low, near_high, far, near),
         *given,
         state=[query] + state,
     )

time: 78.2 us -> 79.4 us (1.015)
  the two profiles are of different devices: /device:TPU:120 before, /device:TPU:384 now
where the time goes in v3:
time: 79.4 us; the launch traced here: 79 us
  starting transfers between devices  39.8 us (50%)
  Pallas kernels  19.9 us (25%)
  waiting for transfers between devices  16.2 us (20%)
  local copies, waits for them, and re-layouts  2.49 us (3%)
    ppermute x10, starting transfers between devices, shifted(): lax.ppermute(block, axis, [((i - distance) % count, i) for i in range(cou...  39.8 us
    pallas_call x3, Pallas kernels, stage(): pl.pallas_call(functools.partial(stage_kernel, layout, kernel, cells, fir...  17.2 us
    ppermute x10, waiting for transfers between devices, shifted(): lax.ppermute(block, axis, [((i - distance) % count, i) for i in range(cou...  16.2 us
    pallas_call x1, Pallas kernels, split_weights(): pl.pallas_call(functools.partial(weight_kernel, head_dim), out_shape=[one...  2.69 us
  transfers between devices with their start and end apart: 10, of which 3 were waited for; matrix products, arithmetic and copies ran while one was open for 3% of the time, Pallas kernels for 18%

profile of v3, /device:TPU:384, one launch (start us, length us, event | category | flops | bytes accessed | tf_op | source)
XLA Modules:
  0.0 79.0 jit_solution(4476015107338580284)
XLA Ops:
  0.0 1.9 %collective-permute-start = (bf16[2,128,512]{2,1,0:T(8,128)(2,1)}, bf16[2,128,512]{2,1,0:T(8,128)(2,1)S(1)}, u32[]{:S(2)}, u32[]{:S(2)}) collective-permute-start(bf16[2,128,512]{2,1,0:T(8,128)(2,1)} %bitcast.11), channel_id=1, source_target_pairs={{448,0},{464,16},{480,32},{496,48},{0,64},{16,80},{32,96},{48,112}... | collective-permute-start | bytes 786440 | tf_op jit(solution)/shard_map/ppermute | solution.py:27
  1.9 3.5 %collective-permute-start.6 = (bf16[2,128,512]{2,1,0:T(8,128)(2,1)}, bf16[2,128,512]{2,1,0:T(8,128)(2,1)S(1)}, u32[]{:S(2)}, u32[]{:S(2)}) collective-permute-start(bf16[2,128,512]{2,1,0:T(8,128)(2,1)} %bitcast.12), channel_id=1, source_target_pairs={{15,0},{0,1},{1,2},{2,3},{3,4},{4,5},{5,6},{6,7},{7,8},{8,9},{9,10... | collective-permute-start | bytes 786440 | tf_op jit(solution)/shard_map/ppermute | solution.py:27
  5.4 4.7 %collective-permute-start.7 = (bf16[2,128,512]{2,1,0:T(8,128)(2,1)}, bf16[2,128,512]{2,1,0:T(8,128)(2,1)S(1)}, u32[]{:S(2)}, u32[]{:S(2)}) collective-permute-start(bf16[2,128,512]{2,1,0:T(8,128)(2,1)} %bitcast.13), channel_id=1, source_target_pairs={{1,0},{2,1},{3,2},{4,3},{5,4},{6,5},{7,6},{8,7},{9,8},{10,9},{11,1... | collective-permute-start | bytes 786440 | tf_op jit(solution)/shard_map/ppermute | solution.py:27
  10.2 4.8 %collective-permute-start.2 = (bf16[2,128,512]{2,1,0:T(8,128)(2,1)}, bf16[2,128,512]{2,1,0:T(8,128)(2,1)S(1)}, u32[]{:S(2)}, u32[]{:S(2)}) collective-permute-start(bf16[2,128,512]{2,1,0:T(8,128)(2,1)} %bitcast.14), channel_id=1, source_target_pairs={{64,0},{80,16},{96,32},{112,48},{128,64},{144,80},{160,96},{176,11... | collective-permute-start | bytes 786440 | tf_op jit(solution)/shard_map/ppermute | solution.py:27
  15.0 1.7 %collective-permute-done = bf16[2,128,512]{2,1,0:T(8,128)(2,1)S(1)} collective-permute-done((bf16[2,128,512]{2,1,0:T(8,128)(2,1)}, bf16[2,128,512]{2,1,0:T(8,128)(2,1)S(1)}, u32[]{:S(2)}, u32[]{:S(2)}) %collective-permute-start) | collective-permute-done | bytes 262176 | tf_op jit(solution)/shard_map/ppermute | solution.py:27
  16.7 7.0 %collective-permute-start.1 = (bf16[2,128,512]{2,1,0:T(8,128)(2,1)S(1)}, bf16[2,128,512]{2,1,0:T(8,128)(2,1)}, u32[]{:S(2)}, u32[]{:S(2)}) collective-permute-start(bf16[2,128,512]{2,1,0:T(8,128)(2,1)S(1)} %collective-permute-done), channel_id=1, source_target_pairs={{448,0},{464,16},{480,32},{496,48},{0,64},{16,80},{32,96},{48,112}... | collective-permute-start | bytes 786440 | tf_op jit(solution)/shard_map/ppermute | solution.py:27
  23.7 2.7 %split_weights.1 = (bf16[512,512]{1,0:T(8,128)(2,1)S(1)}, bf16[512,512]{1,0:T(8,128)(2,1)S(1)}, bf16[512,512]{1,0:T(8,128)(2,1)S(1)}) custom-call(bf16[512,1536]{1,0:T(8,128)(2,1)} %w_ref.1), custom_call_target="tpu_custom_call" | custom-call | flops 3000000000 | bytes 3000000 | tf_op jit(solution)/shard_map/split_weights/pallas_call | solution.py:49
  26.4 0.0 copy-start.3
  26.4 0.0 copy-start.4
  26.4 1.1 %reshape.21 = f32[4,4,5,25]{1,0,3,2:T(4,128)S(1)} reshape(f32[16,5,5,5]{0,3,2,1:T(8,128)} %param.10) | data formatting | bytes 16000 | tf_op jit(solution)/shard_map/reshape | solution.py:75
  27.5 0.2 copy.9
  27.8 0.1 reshape.18
  27.9 2.3 %collective-permute-done.2 = bf16[2,128,512]{2,1,0:T(8,128)(2,1)S(1)} collective-permute-done((bf16[2,128,512]{2,1,0:T(8,128)(2,1)}, bf16[2,128,512]{2,1,0:T(8,128)(2,1)S(1)}, u32[]{:S(2)}, u32[]{:S(2)}) %collective-permute-start.2) | collective-permute-done | bytes 262176 | tf_op jit(solution)/shard_map/ppermute | solution.py:27
  30.2 1.9 %collective-permute-start.3 = (bf16[2,128,512]{2,1,0:T(8,128)(2,1)S(1)}, bf16[2,128,512]{2,1,0:T(8,128)(2,1)S(1)}, u32[]{:S(2)}, u32[]{:S(2)}) collective-permute-start(bf16[2,128,512]{2,1,0:T(8,128)(2,1)S(1)} %collective-permute-done.2), channel_id=1, source_target_pairs={{64,0},{80,16},{96,32},{112,48},{128,64},{144,80},{160,96},{176,11... | collective-permute-start | bytes 786440 | tf_op jit(solution)/shard_map/ppermute | solution.py:27
  32.1 1.9 %collective-permute-start.8 = (bf16[4,128,512]{2,1,0:T(8,128)(2,1)S(1)}, bf16[4,128,512]{2,1,0:T(8,128)(2,1)S(1)}, u32[]{:S(2)}, u32[]{:S(2)}) collective-permute-start(bf16[4,128,512]{2,1,0:T(8,128)(2,1)S(1)} %constant_dynamic-update-slice_fusion.2.refs_3_), channel_id=1, source_target_pairs={{15,0},{0,1},{1,2},{2,3},{3,4},{4,5},{5,6},{6,7},{7,8},{8,9},{9,10... | collective-permute-start | bytes 1572872 | tf_op jit(solution)/shard_map/ppermute | solution.py:27
  34.1 6.0 %collective-permute-start.9 = (bf16[4,128,512]{2,1,0:T(8,128)(2,1)S(1)}, bf16[4,128,512]{2,1,0:T(8,128)(2,1)S(1)}, u32[]{:S(2)}, u32[]{:S(2)}) collective-permute-start(bf16[4,128,512]{2,1,0:T(8,128)(2,1)S(1)} %constant_dynamic-update-slice_fusion.2.refs_3_), channel_id=1, source_target_pairs={{1,0},{2,1},{3,2},{4,3},{5,4},{6,5},{7,6},{8,7},{9,8},{10,9},{11,1... | collective-permute-start | bytes 1572872 | tf_op jit(solution)/shard_map/ppermute | solution.py:27
  40.1 1.0 %constant_dynamic-update-slice_fusion.1 = bf16[4,128,512]{2,1,0:T(8,128)(2,1)S(1)} fusion(bf16[2,128,512]{2,1,0:T(8,128)(2,1)} %collective-permute-done.1), kind=kLoop, calls=%fused_computation.4 | loop fusion | bytes 524288
  41.1 12.2 %collective-permute-done.3 = bf16[2,128,512]{2,1,0:T(8,128)(2,1)S(1)} collective-permute-done((bf16[2,128,512]{2,1,0:T(8,128)(2,1)S(1)}, bf16[2,128,512]{2,1,0:T(8,128)(2,1)S(1)}, u32[]{:S(2)}, u32[]{:S(2)}) %collective-permute-start.3) | collective-permute-done | bytes 262176 | tf_op jit(solution)/shard_map/ppermute | solution.py:27
  53.4 1.9 %collective-permute-start.4 = (bf16[4,128,512]{2,1,0:T(8,128)(2,1)S(1)}, bf16[4,128,512]{2,1,0:T(8,128)(2,1)S(1)}, u32[]{:S(2)}, u32[]{:S(2)}) collective-permute-start(bf16[4,128,512]{2,1,0:T(8,128)(2,1)S(1)} %constant_dynamic-update-slice_fusion.refs_2_), channel_id=1, source_target_pairs={{15,0},{0,1},{1,2},{2,3},{3,4},{4,5},{5,6},{6,7},{7,8},{8,9},{9,10... | collective-permute-start | bytes 1572872 | tf_op jit(solution)/shard_map/ppermute | solution.py:27
  55.3 6.0 %collective-permute-start.5 = (bf16[4,128,512]{2,1,0:T(8,128)(2,1)S(1)}, bf16[4,128,512]{2,1,0:T(8,128)(2,1)S(1)}, u32[]{:S(2)}, u32[]{:S(2)}) collective-permute-start(bf16[4,128,512]{2,1,0:T(8,128)(2,1)S(1)} %constant_dynamic-update-slice_fusion.refs_2_), channel_id=1, source_target_pairs={{1,0},{2,1},{3,2},{4,3},{5,4},{6,5},{7,6},{8,7},{9,8},{10,9},{11,1... | collective-permute-start | bytes 1572872 | tf_op jit(solution)/shard_map/ppermute | solution.py:27
  61.3 0.3 fusion.1.refs_5_.refs_6_.refs_4_
  61.7 5.2 %shard_map.73 = (bf16[4,8,256,128]{3,2,1,0:T(8,128)(2,1)S(1)}, f32[4,256,128]{2,1,0:T(8,128)S(1)}, f32[4,8,128]{2,1,0:T(8,128)S(1)}, f32[4,8,128]{2,1,0:T(8,128)S(1)}) custom-call(bf16[2,128,512]{2,1,0:T(8,128)(2,1)S(1)} %bitcast.15, bf16[2,128,512]{2,1,0:T(8,128)(2,1)S(1)} %collective-permute-done.6.refs_1_, ...), custom_call_target="tpu_custom_call" | custom-call | flops 1500000000 | bytes 3900000 | tf_op jit(solution)/shard_map/pallas_call | solution.py:319
  66.9 6.6 %shard_map.74 = (f32[4,256,128]{2,1,0:T(8,128)S(1)}, f32[4,8,128]{2,1,0:T(8,128)S(1)}, f32[4,8,128]{2,1,0:T(8,128)S(1)}) custom-call(bf16[4,128,512]{2,1,0:T(8,128)(2,1)S(1)} %collective-permute-done.8.refs_0_, bf16[4,128,512]{2,1,0:T(8,128)(2,1)S(1)} %collective-permute-done.9.refs_1_, bf16[4,128,512]{2,1,0:T(8,128)(2,1)S(1)} %constant_dynamic-update-slice_fusion.refs_2_, ...), custom_call_target="tpu_custom_call" | custom-call | flops 4000000000 | bytes 10400000 | tf_op jit(solution)/shard_map/pallas_call | solution.py:319
  73.5 5.5 %shard_map.75 = bf16[2,128,512]{2,1,0:T(8,128)(2,1)} custom-call(bf16[4,128,512]{2,1,0:T(8,128)(2,1)S(1)} %collective-permute-done.4.refs_0_, bf16[4,128,512]{2,1,0:T(8,128)(2,1)S(1)} %collective-permute-done.5.refs_1_, bf16[512,512]{1,0:T(8,128)(2,1)S(1)} %get-tuple-element.15.refs_3_.refs_4_.refs_2_, ...), custom_call_target="tpu_custom_call" | custom-call | flops 2000000000 | bytes 5200000 | tf_op jit(solution)/shard_map/pallas_call | solution.py:319
  (18 shorter events, 0.1 us)
Async XLA Ops:
  0.0 16.7 %collective-permute-start = (bf16[2,128,512]{2,1,0:T(8,128)(2,1)}, bf16[2,128,512]{2,1,0:T(8,128)(2,1)S(1)}, u32[]{:S(2)}, u32[]{:S(2)}) collective-permute-start(bf16[2,128,512]{2,1,0:T(8,128)(2,1)} %bitcast.11), channel_id=1, source_target_pairs={{448,0},{464,16},{480,32},{496,48},{0,64},{16,80},{32,96},{48,112}... | collective-permute-start | bytes 786440 | tf_op jit(solution)/shard_map/ppermute | solution.py:27
  1.9 53.4 %collective-permute-start.6 = (bf16[2,128,512]{2,1,0:T(8,128)(2,1)}, bf16[2,128,512]{2,1,0:T(8,128)(2,1)S(1)}, u32[]{:S(2)}, u32[]{:S(2)}) collective-permute-start(bf16[2,128,512]{2,1,0:T(8,128)(2,1)} %bitcast.12), channel_id=1, source_target_pairs={{15,0},{0,1},{1,2},{2,3},{3,4},{4,5},{5,6},{6,7},{7,8},{8,9},{9,10... | collective-permute-start | bytes 786440 | tf_op jit(solution)/shard_map/ppermute | solution.py:27
  5.4 56.2 %collective-permute-start.7 = (bf16[2,128,512]{2,1,0:T(8,128)(2,1)}, bf16[2,128,512]{2,1,0:T(8,128)(2,1)S(1)}, u32[]{:S(2)}, u32[]{:S(2)}) collective-permute-start(bf16[2,128,512]{2,1,0:T(8,128)(2,1)} %bitcast.13), channel_id=1, source_target_pairs={{1,0},{2,1},{3,2},{4,3},{5,4},{6,5},{7,6},{8,7},{9,8},{10,9},{11,1... | collective-permute-start | bytes 786440 | tf_op jit(solution)/shard_map/ppermute | solution.py:27
  10.2 20.0 %collective-permute-start.2 = (bf16[2,128,512]{2,1,0:T(8,128)(2,1)}, bf16[2,128,512]{2,1,0:T(8,128)(2,1)S(1)}, u32[]{:S(2)}, u32[]{:S(2)}) collective-permute-start(bf16[2,128,512]{2,1,0:T(8,128)(2,1)} %bitcast.14), channel_id=1, source_target_pairs={{64,0},{80,16},{96,32},{112,48},{128,64},{144,80},{160,96},{176,11... | collective-permute-start | bytes 786440 | tf_op jit(solution)/shard_map/ppermute | solution.py:27
  16.7 17.4 %collective-permute-start.1 = (bf16[2,128,512]{2,1,0:T(8,128)(2,1)S(1)}, bf16[2,128,512]{2,1,0:T(8,128)(2,1)}, u32[]{:S(2)}, u32[]{:S(2)}) collective-permute-start(bf16[2,128,512]{2,1,0:T(8,128)(2,1)S(1)} %collective-permute-done), channel_id=1, source_target_pairs={{448,0},{464,16},{480,32},{496,48},{0,64},{16,80},{32,96},{48,112}... | collective-permute-start | bytes 786440 | tf_op jit(solution)/shard_map/ppermute | solution.py:27
  26.4 34.9 %copy-start.3 = (f32[100,768]{1,0:T(8,128)S(1)}, f32[100,768]{1,0:T(8,128)}, u32[]{:S(2)}) copy-start(f32[100,768]{1,0:T(8,128)} %constant.6.clone) | copy-start | bytes 921604
  26.4 34.9 %copy-start.4 = (f32[768]{0:T(1024)S(1)}, f32[768]{0:T(1024)}, u32[]{:S(2)}) copy-start(f32[768]{0:T(1024)} %constant.7.clone) | copy-start | bytes 9220
  26.4 35.3 %copy-start.1 = (bf16[1,2,2,64,512]{4,3,2,1,0:T(8,128)(2,1)S(1)}, bf16[1,2,2,64,512]{4,3,2,1,0:T(8,128)(2,1)}, u32[]{:S(2)}) copy-start(bf16[1,2,2,64,512]{4,3,2,1,0:T(8,128)(2,1)} %param.7) | copy-start | bytes 786436
  30.2 23.2 %collective-permute-start.3 = (bf16[2,128,512]{2,1,0:T(8,128)(2,1)S(1)}, bf16[2,128,512]{2,1,0:T(8,128)(2,1)S(1)}, u32[]{:S(2)}, u32[]{:S(2)}) collective-permute-start(bf16[2,128,512]{2,1,0:T(8,128)(2,1)S(1)} %collective-permute-done.2), channel_id=1, source_target_pairs={{64,0},{80,16},{96,32},{112,48},{128,64},{144,80},{160,96},{176,11... | collective-permute-start | bytes 786440 | tf_op jit(solution)/shard_map/ppermute | solution.py:27
  32.1 34.7 %collective-permute-start.8 = (bf16[4,128,512]{2,1,0:T(8,128)(2,1)S(1)}, bf16[4,128,512]{2,1,0:T(8,128)(2,1)S(1)}, u32[]{:S(2)}, u32[]{:S(2)}) collective-permute-start(bf16[4,128,512]{2,1,0:T(8,128)(2,1)S(1)} %constant_dynamic-update-slice_fusion.2.refs_3_), channel_id=1, source_target_pairs={{15,0},{0,1},{1,2},{2,3},{3,4},{4,5},{5,6},{6,7},{7,8},{8,9},{9,10... | collective-permute-start | bytes 1572872 | tf_op jit(solution)/shard_map/ppermute | solution.py:27
  34.1 32.8 %collective-permute-start.9 = (bf16[4,128,512]{2,1,0:T(8,128)(2,1)S(1)}, bf16[4,128,512]{2,1,0:T(8,128)(2,1)S(1)}, u32[]{:S(2)}, u32[]{:S(2)}) collective-permute-start(bf16[4,128,512]{2,1,0:T(8,128)(2,1)S(1)} %constant_dynamic-update-slice_fusion.2.refs_3_), channel_id=1, source_target_pairs={{1,0},{2,1},{3,2},{4,3},{5,4},{6,5},{7,6},{8,7},{9,8},{10,9},{11,1... | collective-permute-start | bytes 1572872 | tf_op jit(solution)/shard_map/ppermute | solution.py:27
  53.4 20.1 %collective-permute-start.4 = (bf16[4,128,512]{2,1,0:T(8,128)(2,1)S(1)}, bf16[4,128,512]{2,1,0:T(8,128)(2,1)S(1)}, u32[]{:S(2)}, u32[]{:S(2)}) collective-permute-start(bf16[4,128,512]{2,1,0:T(8,128)(2,1)S(1)} %constant_dynamic-update-slice_fusion.refs_2_), channel_id=1, source_target_pairs={{15,0},{0,1},{1,2},{2,3},{3,4},{4,5},{5,6},{6,7},{7,8},{8,9},{9,10... | collective-permute-start | bytes 1572872 | tf_op jit(solution)/shard_map/ppermute | solution.py:27
  55.3 18.2 %collective-permute-start.5 = (bf16[4,128,512]{2,1,0:T(8,128)(2,1)S(1)}, bf16[4,128,512]{2,1,0:T(8,128)(2,1)S(1)}, u32[]{:S(2)}, u32[]{:S(2)}) collective-permute-start(bf16[4,128,512]{2,1,0:T(8,128)(2,1)S(1)} %constant_dynamic-update-slice_fusion.refs_2_), channel_id=1, source_target_pairs={{1,0},{2,1},{3,2},{4,3},{5,4},{6,5},{7,6},{8,7},{9,8},{10,9},{11,1... | collective-permute-start | bytes 1572872 | tf_op jit(solution)/shard_map/ppermute | solution.py:27
  66.9 6.6 %copy-start = (bf16[512,512]{1,0:T(8,128)(2,1)S(1)}, bf16[512,512]{1,0:T(8,128)(2,1)}, u32[]{:S(2)}) copy-start(bf16[512,512]{1,0:T(8,128)(2,1)} %refs_9_.1) | copy-start | bytes 1572868
  66.9 6.6 %copy-start.2 = (f32[512]{0:T(512)S(1)}, f32[512]{0:T(512)}, u32[]{:S(2)}) copy-start(f32[512]{0:T(512)} %param.11) | copy-start | bytes 6148
